TPU v7x, 128 devices: a whole 4x4x4 slice. The times are simulated.
128 devices in a mesh: rx: 8 (over x, core), ry: 16 (over y, z).
Axes of the slice: x: 4, y: 4, z: 4, core: 2. Of those that a mesh axis runs over, the one named last changes fastest.
Arguments:
- column_features: bfloat16 [16384, 1536], P(('rx', 'ry')), may hold values from -6 to 6
- column_route: int32 [16384], P(('rx', 'ry')), may hold values from 0 to 32767, as said below
- cotangent: bfloat16 [128, 256, 1536], P('rx', 'ry'), may hold values from -6 to 6
- first_weight: bfloat16 [27, 96, 96], replicated, may hold values from -0.125 to 0.125
- second_weight: bfloat16 [27, 96, 96], replicated, may hold values from -0.125 to 0.125
Outputs:
- block_output: bfloat16 [128, 256, 1536], P('rx', 'ry')
- feature_grads: bfloat16 [16384, 1536], P(('rx', 'ry'))
- first_grad: float32 [27, 96, 96], replicated
- second_grad: float32 [27, 96, 96], replicated
Inputs may be any that keep to these rules, and one draw needn't show every extreme that they name: `column_route`: entries are distinct; entry o * 256 + q names slot q of owner o, owner o = i * 16 + j being the device at rx index i and ry index j. The columns of one owner are spread over the devices' shards as evenly as possible: each shard holds the floor or the ceiling of that owner's count / 128. An owner holds at most 256 columns, and in every draw one owner holds exactly 256, so that it receives 2 from every shard.
All inputs are finite; a program needn't handle non-finite values.
Results may differ from a plain program's by a relative error of at most 0.0029.
Values may be sent and summed in bfloat16 or wider, within the bound.
A program may use at most 256 MiB of HBM per device.

v0:
```python
import jax
import jax.numpy as jnp
from jax import lax
from jax.sharding import PartitionSpec as P


def extended(block, sides, width):
    for axis, dim in sides:
        count = lax.axis_size(axis)
        forward = [(i, i + 1) for i in range(count - 1)]
        backward = [(target, source) for source, target in forward]
        low = lax.ppermute(
            lax.slice_in_dim(block, block.shape[dim] - width, None, axis=dim), axis, forward
        )
        high = lax.ppermute(lax.slice_in_dim(block, 0, width, axis=dim), axis, backward)
        block = jnp.concatenate([low, block, high], axis=dim)
    return block


def pad_depth(widened, channels):
    shaped = widened.reshape(
        widened.shape[0], widened.shape[1], widened.shape[2] // channels, channels
    )
    return jnp.pad(shaped, ((0, 0), (0, 0), (1, 1), (0, 0)))


def face_field(rows, channels):
    widened = extended(rows, (("rx", 0), ("ry", 1)), 1)
    return pad_depth(widened, channels)


def conv_sum(padded, weights):
    size_x = padded.shape[0] - 2
    size_y = padded.shape[1] - 2
    size_z = padded.shape[2] - 2
    result = jnp.zeros((size_x, size_y, size_z, weights.shape[1]), jnp.float32)
    for a in range(3):
        for b in range(3):
            for c in range(3):
                piece = padded[a : a + size_x, b : b + size_y, c : c + size_z, :]
                result = result + jnp.einsum(
                    "xyzi,oi->xyzo",
                    piece,
                    weights[9 * a + 3 * b + c],
                    preferred_element_type=jnp.float32,
                )
    return result


def correlate(grads, padded):
    size_x, size_y, size_z, _ = grads.shape
    terms = []
    for a in range(3):
        for b in range(3):
            for c in range(3):
                piece = padded[a : a + size_x, b : b + size_y, c : c + size_z, :]
                terms.append(
                    jnp.einsum("xyzo,xyzi->oi", grads, piece, preferred_element_type=jnp.float32)
                )
    return jnp.stack(terms, axis=0)


def flipped(weights):
    return jnp.transpose(weights[::-1], (0, 2, 1))


def on_device(column_features, column_route, cotangent, first_weight, second_weight):
    count_x = lax.axis_size("rx")
    count_y = lax.axis_size("ry")
    count_all = count_x * count_y
    shard_rows = column_features.shape[0]
    row_width = column_features.shape[1]
    region_x = cotangent.shape[0]
    region_y = cotangent.shape[1]
    channels = first_weight.shape[1]
    depth = row_width // channels
    region_slots = region_x * region_y
    capacity = 2 * shard_rows // count_all
    owners = column_route // region_slots
    slot_ids = column_route % region_slots
    shard_index = jnp.arange(shard_rows, dtype=jnp.int32)
    earlier = shard_index[:, None] > shard_index[None, :]
    same_owner = owners[:, None] == owners[None, :]
    ranks = jnp.sum(jnp.logical_and(earlier, same_owner).astype(jnp.int32), axis=1)
    send_pos = owners * capacity + ranks
    buffer_index = jnp.arange(count_all * capacity, dtype=jnp.int32)
    send_hot = send_pos[:, None] == buffer_index[None, :]
    send_table = send_hot.astype(jnp.bfloat16)
    outgoing = jnp.einsum(
        "sr,sw->rw", send_table, column_features, preferred_element_type=jnp.float32
    ).astype(jnp.bfloat16)
    filled = jnp.sum(send_hot.astype(jnp.int32), axis=0)
    slot_total = jnp.sum(jnp.where(send_hot, slot_ids[:, None], 0), axis=0)
    out_slots = jnp.where(filled > 0, slot_total, region_slots)
    incoming, in_slots = (
        lax.all_to_all(
            outgoing.reshape(count_all, capacity, row_width),
            ("rx", "ry"),
            split_axis=0,
            concat_axis=0,
            tiled=True,
        ),
        lax.all_to_all(
            out_slots.reshape(count_all, capacity),
            ("rx", "ry"),
            split_axis=0,
            concat_axis=0,
            tiled=True,
        ),
    )
    incoming = incoming.reshape(count_all * capacity, row_width)
    in_slots = in_slots.reshape(count_all * capacity)
    slot_hot = in_slots[:, None] == jnp.arange(region_slots, dtype=jnp.int32)[None, :]
    slot_table = slot_hot.astype(jnp.bfloat16)
    region_rows = jnp.einsum(
        "rs,rw->sw", slot_table, incoming, preferred_element_type=jnp.float32
    ).astype(jnp.bfloat16)
    active = jnp.sum(slot_hot.astype(jnp.float32), axis=0)
    field = jnp.transpose(region_rows.reshape(region_x, region_y, channels, depth), (0, 1, 3, 2))
    mask = active.reshape(region_x, region_y, 1, 1)
    cot_field = jnp.transpose(
        cotangent.reshape(region_x, region_y, channels, depth), (0, 1, 3, 2)
    ).astype(jnp.float32)
    outer_grad = (mask * cot_field).astype(jnp.bfloat16)
    field_flat = field.reshape(region_x, region_y, row_width)
    outer_flat = outer_grad.reshape(region_x, region_y, row_width)
    padded_x = pad_depth(extended(field_flat, (("rx", 0), ("ry", 1)), 1), channels)
    padded_g = pad_depth(extended(outer_flat, (("rx", 0), ("ry", 1)), 1), channels)
    hidden = mask * conv_sum(padded_x, first_weight)
    act = jax.nn.silu(hidden).astype(jnp.bfloat16)
    padded_a = face_field(act.reshape(region_x, region_y, row_width), channels)
    second = conv_sum(padded_a, second_weight)
    summed = (field.astype(jnp.float32) + mask * second).astype(jnp.bfloat16)
    block_output = jnp.transpose(summed, (0, 1, 3, 2)).reshape(region_x, region_y, row_width)
    act_grad = conv_sum(padded_g, flipped(second_weight))
    sigma = jax.nn.sigmoid(hidden)
    hidden_grad = (mask * act_grad * sigma * (1.0 + hidden * (1.0 - sigma))).astype(jnp.bfloat16)
    padded_h = face_field(hidden_grad.reshape(region_x, region_y, row_width), channels)
    grid_grad = (mask * cot_field + conv_sum(padded_h, flipped(first_weight))).astype(jnp.bfloat16)
    grad_rows = jnp.transpose(grid_grad, (0, 1, 3, 2)).reshape(region_slots, row_width)
    backward = jnp.dot(slot_table, grad_rows, preferred_element_type=jnp.float32).astype(
        jnp.bfloat16
    )
    returned = lax.all_to_all(
        backward.reshape(count_all, capacity, row_width),
        ("rx", "ry"),
        split_axis=0,
        concat_axis=0,
        tiled=True,
    )
    returned_rows = returned.reshape(count_all * capacity, row_width)
    feature_grads = jnp.dot(send_table, returned_rows, preferred_element_type=jnp.float32).astype(
        jnp.bfloat16
    )
    second_local = correlate(outer_grad, padded_a)
    first_local = correlate(hidden_grad, padded_x)
    first_total, second_total = lax.psum((first_local, second_local), ("rx", "ry"))
    factor = 1.0 / jnp.sqrt(jnp.float32(count_all * shard_rows * depth))
    return (block_output, feature_grads, first_total * factor, second_total * factor)


def solution(mesh):
    in_specs = (P(("rx", "ry"), None), P(("rx", "ry")), P("rx", "ry", None), P(), P())
    out_specs = (P("rx", "ry", None), P(("rx", "ry"), None), P(), P())
    return jax.shard_map(
        on_device, mesh=mesh, in_specs=in_specs, out_specs=out_specs, check_vma=False
    )
```

profile of v0, /device:TPU:1, one launch (start us, length us, event | category | flops | bytes accessed | tf_op | source)
XLA Modules:
  0.0 670.0 jit_solution(15882649967225699093)
XLA Ops:
  9.0 11.5 %all-to-all-start = ((s32[128,1,2]{2,1,0:T(1,128)}), s32[128,1,2]{2,1,0:T(1,128)S(1)}, u32[]{:S(2)}, u32[]{:S(2)}) async-start(s32[128,1,2]{2,1,0:T(1,128)} %bitcast), calls=%async_computation | async-start | bytes 131072 | tf_op jit(solution)/shard_map/all_to_all | solution.py:103
  24.4 6.9 %reshape.118 = f32[16,16,96,16]{3,2,1,0:T(8,128)} reshape(bf16[16,16,1536]{2,1,0:T(8,128)(2,1)S(1)} %copy-done.16) | data formatting | bytes 2359296 | tf_op jit(solution)/shard_map/convert_element_type | solution.py:123
  31.2 8.4 %copy.37 = f32[16,16,96,16]{2,3,1,0:T(8,128)S(1)} copy(f32[16,16,96,16]{3,2,1,0:T(8,128)} %reshape.118) | data formatting | bytes 3145728 | tf_op jit(solution)/shard_map/convert_element_type | solution.py:123
  39.7 10.2 %all-to-all-start.1 = ((bf16[128,2,1536]{2,1,0:T(2,128)(2,1)}), bf16[128,2,1536]{2,1,0:T(2,128)(2,1)}, u32[]{:S(2)}, u32[]{:S(2)}) async-start(bf16[128,2,1536]{2,1,0:T(2,128)(2,1)} %reshape.103), calls=%async_computation.1 | async-start | bytes 1572864 | tf_op jit(solution)/shard_map/all_to_all | solution.py:96
  52.0 3.5 collective-permute-start.8
  62.3 3.8 collective-permute-done.9
  66.3 3.1 collective-permute-start.10
  71.8 3.1 collective-permute-done.11
  123.2 6.8 %reshape.105 = bf16[16,16,96,16]{3,2,1,0:T(8,128)(2,1)} reshape(bf16[256,1536]{1,0:T(8,128)(2,1)S(1)} %convolution_convert_fusion.2) | data formatting | bytes 1572864 | tf_op jit(solution)/shard_map/reshape | solution.py:119
  132.0 3.9 collective-permute-start
  138.5 6.0 copy.34
  150.5 3.4 collective-permute-start.2
  157.7 6.1 copy.32
  165.5 2.7 reshape.107
  168.3 2.6 fusion.114
  215.7 20.1 %multiply_convert_fusion.1 = (bf16[16,16,16,96]{3,2,1,0:T(8,128)(2,1)}, f32[16,16,16,96]{3,2,1,0:T(8,128)}) fusion(bf16[27,96,96]{2,1,0:T(8,128)(2,1)} %param.8, bf16[18,18,16,96]{3,2,1,0:T(8,128)(2,1)S(1)} %reshape.107, f32[16,16,16,96]{3,2,1,0:T(8,128)} %fusion.208, f32[16,16,16,96]{3,2,1,0:T(8,128)} %fusion.129, f32[16,16,16,96]{3,2,1,0:T(8,128)} %fusion.128, ...), kind=kOutput, calls=%fused_computation.102 | convolution fusion | flops 88080384 | bytes 57906176 | tf_op jit(solution)/shard_map/xyzi,oi->xyzo/dot_general | solution.py:41
  235.8 20.1 %multiply_convert_fusion = bf16[16,16,16,96]{3,2,1,0:T(8,128)(2,1)} fusion(f32[16,16,16,96]{3,2,1,0:T(8,128)} %get-tuple-element.27, f32[16,16,16,96]{3,2,1,0:T(8,128)} %fusion.162, f32[16,16,16,96]{3,2,1,0:T(8,128)} %fusion.76, f32[16,16,16,96]{3,2,1,0:T(8,128)} %fusion.75, f32[16,16,16,96]{3,2,1,0:T(8,128)} %fusion.163, f32[16,16,16,96]{3,2,1,0:T(8,128)} %fusion.74, ...), kind=kOutput, calls=%fused_computation.101 | convolution fusion | flops 89653248 | bytes 58430464 | tf_op jit(solution)/shard_map/xyzi,oi->xyzo/dot_general | solution.py:41
  262.0 3.2 collective-permute-start.12
  304.0 4.0 collective-permute-start.6
  309.6 4.9 collective-permute-start.14
  317.6 2.6 fusion.132
  367.8 2.9 reshape.114
  370.7 2.6 fusion.79
  447.1 19.9 %fusion.1 = bf16[16,16,96,16]{2,3,1,0:T(8,128)(2,1)} fusion(f32[16,16,16,96]{3,2,1,0:T(8,128)} %fusion.153, f32[16,16,16,96]{3,2,1,0:T(8,128)} %fusion.94, f32[16,16,16,96]{3,2,1,0:T(8,128)} %fusion.93, f32[16,16,16,96]{3,2,1,0:T(8,128)} %fusion.154, f32[16,16,16,96]{3,2,1,0:T(8,128)} %fusion.92, f32[16,16,16,96]{3,2,1,0:T(8,128)} %fusion.91, ...), kind=kOutput, calls=%fused_computation.78 | convolution fusion | flops 86900736 | bytes 58430464 | tf_op jit(solution)/shard_map/xyzi,oi->xyzo/dot_general | solution.py:41
  466.9 6.0 copy.40
  472.9 11.3 %reshape.115 = bf16[256,1536]{1,0:T(8,128)(2,1)S(1)} reshape(bf16[16,16,96,16]{3,2,1,0:T(8,128)(2,1)} %copy.40) | data formatting | bytes 1572864 | tf_op jit(solution)/shard_map/reshape | solution.py:140
  485.9 13.1 %all-to-all-start.2 = ((bf16[128,2,1536]{2,1,0:T(2,128)(2,1)}), bf16[128,2,1536]{2,1,0:T(2,128)(2,1)S(1)}, u32[]{:S(2)}, u32[]{:S(2)}) async-start(bf16[128,2,1536]{2,1,0:T(2,128)(2,1)} %reshape.116), calls=%async_computation.2 | async-start | bytes 1572864 | tf_op jit(solution)/shard_map/all_to_all | solution.py:144
  499.8 19.6 %fusion.4 = bf16[16,16,96,16]{2,3,1,0:T(8,128)(2,1)} fusion(f32[16,16,16,96]{3,2,1,0:T(8,128)} %fusion.172, f32[16,16,16,96]{3,2,1,0:T(8,128)} %fusion.147, f32[16,16,16,96]{3,2,1,0:T(8,128)} %fusion.146, f32[16,16,16,96]{3,2,1,0:T(8,128)} %fusion.176, f32[16,16,16,96]{3,2,1,0:T(8,128)} %fusion.145, f32[16,16,16,96]{3,2,1,0:T(8,128)} %fusion.144, ...), kind=kOutput, calls=%fused_computation.91 | convolution fusion | flops 87293952 | bytes 57119744 | tf_op jit(solution)/shard_map/xyzi,oi->xyzo/dot_general | solution.py:41
  519.4 6.0 copy.36
  525.4 11.8 %reshape.110 = bf16[16,16,1536]{2,1,0:T(8,128)(2,1)} reshape(bf16[16,16,96,16]{3,2,1,0:T(8,128)(2,1)} %copy.36) | data formatting | bytes 1572864 | tf_op jit(solution)/shard_map/reshape | solution.py:134
  538.6 120.6 %all-reduce.7.cloned.1.call-done = (f32[27,96,96]{2,1,0:T(8,128)}, f32[27,96,96]{2,1,0:T(8,128)}) async-done(((f32[27,96,96]{2,1,0:T(8,128)}, f32[27,96,96]{2,1,0:T(8,128)}), (f32[27,96,96]{2,1,0:T(8,128)}, f32[27,96,96]{2,1,0:T(8,128)})) %all-reduce.7.cloned.1.call-update) | async-done | bytes 1990672 | tf_op jit(solution)/shard_map/psum | solution.py:157
  659.2 3.5 broadcast_multiply_fusion
  (293 shorter events, 300.5 us)
Async XLA Ops:
  7.2 13.3 %copy-start = (bf16[128,1536]{1,0:T(8,128)(2,1)S(1)}, bf16[128,1536]{1,0:T(8,128)(2,1)}, u32[]{:S(2)}) copy-start(bf16[128,1536]{1,0:T(8,128)(2,1)} %param.5) | copy-start | bytes 1179652
  8.1 16.3 %copy-start.21 = (s32[128]{0:T(128)}, s32[128]{0:T(128)S(1)}, u32[]{:S(2)}) copy-start(s32[128]{0:T(128)S(1)} %multiply_add_fusion) | copy-start | bytes 1540
  9.0 30.7 %all-to-all-start = ((s32[128,1,2]{2,1,0:T(1,128)}), s32[128,1,2]{2,1,0:T(1,128)S(1)}, u32[]{:S(2)}, u32[]{:S(2)}) async-start(s32[128,1,2]{2,1,0:T(1,128)} %bitcast), calls=%async_computation | async-start | bytes 131072 | tf_op jit(solution)/shard_map/all_to_all | solution.py:103
  20.5 3.8 copy-start.16
  39.6 12.2 %copy-start.2 = (f32[16,16,96,16]{2,3,1,0:T(8,128)}, f32[16,16,96,16]{2,3,1,0:T(8,128)S(1)}, u32[]{:S(2)}) copy-start(f32[16,16,96,16]{2,3,1,0:T(8,128)S(1)} %copy.37) | copy-start | bytes 4718596
  39.7 80.8 %all-to-all-start.1 = ((bf16[128,2,1536]{2,1,0:T(2,128)(2,1)}), bf16[128,2,1536]{2,1,0:T(2,128)(2,1)}, u32[]{:S(2)}, u32[]{:S(2)}) async-start(bf16[128,2,1536]{2,1,0:T(2,128)(2,1)} %reshape.103), calls=%async_computation.1 | async-start | bytes 1572864 | tf_op jit(solution)/shard_map/all_to_all | solution.py:96
  51.3 71.4 %copy-start.19 = (s32[256]{0:T(256)}, s32[256]{0:T(256)S(1)}, u32[]{:S(2)}) copy-start(s32[256]{0:T(256)S(1)} %eq.49) | copy-start | bytes 3076
  51.5 6.0 copy-start.17
  51.9 8.3 %copy-start.6 = (bf16[16,16,16,96]{3,2,1,0:T(8,128)(2,1)}, bf16[16,16,16,96]{3,2,1,0:T(8,128)(2,1)S(1)}, u32[]{:S(2)}) copy-start(bf16[16,16,16,96]{3,2,1,0:T(8,128)(2,1)S(1)} %fusion.59) | copy-start | bytes 2359300
  52.0 10.2 %collective-permute-start.8 = (bf16[1,16,1536]{2,1,0:T(8,128)(2,1)S(1)}, bf16[1,16,1536]{2,1,0:T(8,128)(2,1)S(1)}, u32[]{:S(2)}, u32[]{:S(2)}) collective-permute-start(bf16[1,16,1536]{2,1,0:T(8,128)(2,1)S(1)} %slice.931), channel_id=1, source_target_pairs={{0,16},{16,32},{32,48},{48,64},{64,80},{80,96},{96,112},{1,17},{17... | collective-permute-start | bytes 147464 | tf_op jit(solution)/shard_map/ppermute | solution.py:12
  60.3 5.8 collective-permute-start.9
  66.3 5.5 collective-permute-start.10
  69.4 5.5 collective-permute-start.11
  132.0 16.0 %collective-permute-start = (bf16[1,16,1536]{2,1,0:T(8,128)(2,1)}, bf16[1,16,1536]{2,1,0:T(8,128)(2,1)}, u32[]{:S(2)}, u32[]{:S(2)}) collective-permute-start(bf16[1,16,1536]{2,1,0:T(8,128)(2,1)} %slice.811), channel_id=1, source_target_pairs={{0,16},{16,32},{32,48},{48,64},{64,80},{80,96},{96,112},{1,17},{17... | collective-permute-start | bytes 147464 | tf_op jit(solution)/shard_map/ppermute | solution.py:12
  144.9 5.4 collective-permute-start.1
  150.5 13.3 %collective-permute-start.2 = (bf16[18,1,1536]{2,1,0:T(2,128)(2,1)S(1)}, bf16[18,1,1536]{2,1,0:T(2,128)(2,1)S(1)}, u32[]{:S(2)}, u32[]{:S(2)}) collective-permute-start(bf16[18,1,1536]{2,1,0:T(2,128)(2,1)S(1)} %get-tuple-element.22), channel_id=1, source_target_pairs={{0,1},{1,2},{2,3},{3,4},{4,5},{5,6},{6,7},{7,8},{8,9},{9,10},{10,1... | collective-permute-start | bytes 165896 | tf_op jit(solution)/shard_map/ppermute | solution.py:12
  153.8 10.0 %collective-permute-start.3 = (bf16[18,1,1536]{2,1,0:T(2,128)(2,1)S(1)}, bf16[18,1,1536]{2,1,0:T(2,128)(2,1)S(1)}, u32[]{:S(2)}, u32[]{:S(2)}) collective-permute-start(bf16[18,1,1536]{2,1,0:T(2,128)(2,1)S(1)} %get-tuple-element.23), channel_id=1, source_target_pairs={{1,0},{2,1},{3,2},{4,3},{5,4},{6,5},{7,6},{8,7},{9,8},{10,9},{11,1... | collective-permute-start | bytes 165896 | tf_op jit(solution)/shard_map/ppermute | solution.py:15
  259.4 43.0 %collective-permute-start.4 = (bf16[1,16,1536]{2,1,0:T(8,128)(2,1)S(1)}, bf16[1,16,1536]{2,1,0:T(8,128)(2,1)S(1)}, u32[]{:S(2)}, u32[]{:S(2)}) collective-permute-start(bf16[1,16,1536]{2,1,0:T(8,128)(2,1)S(1)} %slice.871), channel_id=1, source_target_pairs={{0,16},{16,32},{32,48},{48,64},{64,80},{80,96},{96,112},{1,17},{17... | collective-permute-start | bytes 147464 | tf_op jit(solution)/shard_map/ppermute | solution.py:12
  262.0 5.5 copy-start.4
  262.0 47.2 %collective-permute-start.12 = (bf16[1,16,1536]{2,1,0:T(8,128)(2,1)S(1)}, bf16[1,16,1536]{2,1,0:T(8,128)(2,1)S(1)}, u32[]{:S(2)}, u32[]{:S(2)}) collective-permute-start(bf16[1,16,1536]{2,1,0:T(8,128)(2,1)S(1)} %slice.991), channel_id=1, source_target_pairs={{0,16},{16,32},{32,48},{48,64},{64,80},{80,96},{96,112},{1,17},{17... | collective-permute-start | bytes 147464 | tf_op jit(solution)/shard_map/ppermute | solution.py:12
  298.4 5.4 collective-permute-start.5
  300.4 8.9 %collective-permute-start.13 = (bf16[1,16,1536]{2,1,0:T(8,128)(2,1)S(1)}, bf16[1,16,1536]{2,1,0:T(8,128)(2,1)S(1)}, u32[]{:S(2)}, u32[]{:S(2)}) collective-permute-start(bf16[1,16,1536]{2,1,0:T(8,128)(2,1)S(1)} %slice.993), channel_id=1, source_target_pairs={{16,0},{32,16},{48,32},{64,48},{80,64},{96,80},{112,96},{17,1},{33... | collective-permute-start | bytes 147464 | tf_op jit(solution)/shard_map/ppermute | solution.py:15
  304.0 11.8 %collective-permute-start.6 = (bf16[18,1,1536]{2,1,0:T(2,128)(2,1)S(1)}, bf16[18,1,1536]{2,1,0:T(2,128)(2,1)S(1)}, u32[]{:S(2)}, u32[]{:S(2)}) collective-permute-start(bf16[18,1,1536]{2,1,0:T(2,128)(2,1)S(1)} %get-tuple-element.20), channel_id=1, source_target_pairs={{0,1},{1,2},{2,3},{3,4},{4,5},{5,6},{6,7},{7,8},{8,9},{9,10},{10,1... | collective-permute-start | bytes 165896 | tf_op jit(solution)/shard_map/ppermute | solution.py:12
  308.0 7.8 %collective-permute-start.7 = (bf16[18,1,1536]{2,1,0:T(2,128)(2,1)S(1)}, bf16[18,1,1536]{2,1,0:T(2,128)(2,1)S(1)}, u32[]{:S(2)}, u32[]{:S(2)}) collective-permute-start(bf16[18,1,1536]{2,1,0:T(2,128)(2,1)S(1)} %get-tuple-element.21), channel_id=1, source_target_pairs={{1,0},{2,1},{3,2},{4,3},{5,4},{6,5},{7,6},{8,7},{9,8},{10,9},{11,1... | collective-permute-start | bytes 165896 | tf_op jit(solution)/shard_map/ppermute | solution.py:15
  309.4 6.4 copy-start.14
  309.6 56.5 %collective-permute-start.14 = (bf16[18,1,1536]{2,1,0:T(2,128)(2,1)S(1)}, bf16[18,1,1536]{2,1,0:T(2,128)(2,1)S(1)}, u32[]{:S(2)}, u32[]{:S(2)}) collective-permute-start(bf16[18,1,1536]{2,1,0:T(2,128)(2,1)S(1)} %get-tuple-element.16), channel_id=1, source_target_pairs={{0,1},{1,2},{2,3},{3,4},{4,5},{5,6},{6,7},{7,8},{8,9},{9,10},{10,1... | collective-permute-start | bytes 165896 | tf_op jit(solution)/shard_map/ppermute | solution.py:12
  314.4 51.6 %collective-permute-start.15 = (bf16[18,1,1536]{2,1,0:T(2,128)(2,1)S(1)}, bf16[18,1,1536]{2,1,0:T(2,128)(2,1)S(1)}, u32[]{:S(2)}, u32[]{:S(2)}) collective-permute-start(bf16[18,1,1536]{2,1,0:T(2,128)(2,1)S(1)} %get-tuple-element.17), channel_id=1, source_target_pairs={{1,0},{2,1},{3,2},{4,3},{5,4},{6,5},{7,6},{8,7},{9,8},{10,9},{11,1... | collective-permute-start | bytes 165896 | tf_op jit(solution)/shard_map/ppermute | solution.py:15
  472.9 11.3 %copy-start.20 = (s32[256]{0:T(256)S(1)}, s32[256]{0:T(256)}, u32[]{:S(2)}) copy-start(s32[256]{0:T(256)} %copy-done.19) | copy-start | bytes 3076
  485.9 13.9 %copy-start.9 = (bf16[16,16,96,16]{2,3,1,0:T(8,128)(2,1)S(1)}, bf16[16,16,96,16]{2,3,1,0:T(8,128)(2,1)}, u32[]{:S(2)}) copy-start(bf16[16,16,96,16]{2,3,1,0:T(8,128)(2,1)} %copy.32) | copy-start | bytes 2359300
  485.9 51.3 %all-to-all-start.2 = ((bf16[128,2,1536]{2,1,0:T(2,128)(2,1)}), bf16[128,2,1536]{2,1,0:T(2,128)(2,1)S(1)}, u32[]{:S(2)}, u32[]{:S(2)}) async-start(bf16[128,2,1536]{2,1,0:T(2,128)(2,1)} %reshape.116), calls=%async_computation.2 | async-start | bytes 1572864 | tf_op jit(solution)/shard_map/all_to_all | solution.py:144
  499.0 160.2 %all-reduce.7.cloned.1.call-start = ((), (), s32[]{:S(2)}) async-start(), calls=%async_computation.3 | async-start | bytes 5308416 | tf_op jit(solution)/shard_map/psum | solution.py:157
  525.4 12.1 %copy-start.22 = (s32[128]{0:T(128)S(1)}, s32[128]{0:T(128)}, u32[]{:S(2)}) copy-start(s32[128]{0:T(128)} %copy-done.21) | copy-start | bytes 1540
  (11 other events, 24.8 us)
Sparse Core Ops, SparseCore 0:
  505.5 153.6 all-reduce.6
where the time goes:
time: 677 us; the launch traced here: 670 us
  matrix products  336 us (50%)
  waiting for transfers between devices  131 us (19%)
  local copies, waits for them, and re-layouts  101 us (15%)
  starting transfers between devices  76.5 us (11%)
  between operations  15.2 us (2%)
  other arithmetic  10.5 us (2%)
    dot_general x108, matrix products, conv_sum(): jnp.einsum('xyzi,oi->xyzo', piece, weights[9 * a + 3 * b + c], preferred_...  270 us
    psum x1, waiting for transfers between devices, on_device(): lax.psum((first_local, second_local), ('rx', 'ry'))  121 us
    dot_general x54, matrix products, correlate(): jnp.einsum('xyzo,xyzi->oi', grads, piece, preferred_element_type=jnp.floa...  63.1 us
    ppermute x8, starting transfers between devices, extended(): lax.ppermute(lax.slice_in_dim(block, block.shape[dim] - width, None, axis...  28.5 us
    convert_element_type x2, local copies, waits for them, and re-layouts, on_device(): cot_field = jnp.transpose(cotangent.reshape(region_x, region_y, channels,...  15.3 us
  transfers between devices with their start and end apart: 20, of which 5 were waited for; matrix products, arithmetic and copies ran while one was open for 32% of the time, Pallas kernels for 0%

commit v1 on v0

v1 whole, which is shorter than its diff:
```python
import functools

import jax
import jax.numpy as jnp
from jax import lax
from jax.experimental import pallas as pl
from jax.experimental.pallas import tpu as pltpu
from jax.sharding import PartitionSpec as P

F32 = jnp.float32
BF16 = jnp.bfloat16
LANES = 128
VMEM_LIMIT = 64 * 1000 * 1000


def params():
    return pltpu.CompilerParams(vmem_limit_bytes=VMEM_LIMIT)


def iota(shape, dim):
    return lax.broadcasted_iota(jnp.int32, shape, dim)


def spread_columns(rows, scratch, put, depth):
    width = rows.shape[1]
    count = rows.shape[0]
    for zp in range(depth // 2):
        k = iota((width, 2 * LANES), 0)
        n = iota((width, 2 * LANES), 1)
        want = (n % LANES) * depth + 2 * zp + n // LANES
        table = jnp.where(k == want, 1.0, 0.0).astype(BF16)
        moved = jnp.dot(rows, table, preferred_element_type=F32)
        scratch[pl.ds(2 * zp, count, stride=depth), :] = moved[:, :LANES]
        scratch[pl.ds(2 * zp + 1, count, stride=depth), :] = moved[:, LANES:]


def gather_columns(scratch, count, depth, width):
    total = jnp.zeros((count, width), F32)
    for zp in range(depth // 2):
        n = iota((2 * LANES, width), 0)
        k = iota((2 * LANES, width), 1)
        want = (n % LANES) * depth + 2 * zp + n // LANES
        table = jnp.where(k == want, 1.0, 0.0).astype(BF16)
        pair = jnp.concatenate(
            [
                scratch[pl.ds(2 * zp, count, stride=depth), :],
                scratch[pl.ds(2 * zp + 1, count, stride=depth), :],
            ],
            axis=1,
        ).astype(BF16)
        total = total + jnp.dot(pair, table, preferred_element_type=F32)
    return total.astype(BF16)


def shift_planes(src, dst):
    count_x, count_y, depth, lanes = src.shape
    z = iota((count_y * depth, lanes), 0) % depth

    def body(x, carry):
        plane = src[x]
        v = plane.astype(F32).reshape(count_y * depth, lanes)
        below = pltpu.roll(v, 1, 0)
        above = pltpu.roll(v, count_y * depth - 1, 0)
        dst[0, x] = jnp.where(z == 0, 0.0, below).astype(BF16).reshape(count_y, depth, lanes)
        dst[1, x] = plane
        dst[2, x] = jnp.where(z == depth - 1, 0.0, above).astype(BF16).reshape(
            count_y, depth, lanes
        )
        return carry

    lax.fori_loop(0, count_x, body, 0)


def pair_weights(weights, table, transposed):
    table[...] = jnp.zeros(table.shape, BF16)
    channels = weights.shape[1]
    for a in range(3):
        for b in range(3):
            for c in range(3):
                tap = 9 * a + 3 * b + c
                if transposed:
                    block = weights[tap].astype(F32).T.astype(BF16)
                else:
                    block = weights[26 - tap]
                for p in range(2):
                    row = ((a + p) * 9 + 3 * b + c) * LANES
                    table[row : row + channels, p * LANES : p * LANES + channels] = block


def pair_patches(planes, xp, count_y):
    depth = planes.shape[3]
    pieces = []
    for j in range(4):
        for b in range(3):
            for c in range(3):
                pieces.append(
                    planes[c, 2 * xp + j, b : b + count_y].reshape(count_y * depth, LANES)
                )
    return jnp.concatenate(pieces, axis=1)


def pair_conv(planes, table, xp, count_y):
    return jnp.dot(
        pair_patches(planes, xp, count_y), table[...], preferred_element_type=F32
    )


def correlate(local, planes, turned, out, flip):
    count_x, count_y, depth, _ = local.shape
    rows = count_y * depth
    for xp in range(count_x // 2):
        pair = jnp.concatenate(
            [
                local[2 * xp].reshape(rows, LANES),
                local[2 * xp + 1].reshape(rows, LANES),
            ],
            axis=1,
        )
        turned[:, xp * rows : (xp + 1) * rows] = pair.astype(F32).T.astype(BF16)
    out[...] = jnp.zeros(out.shape, F32)

    def body(step, carry):
        jj = (step // 3) * 2
        b = step % 3
        pieces = []
        for dj in range(2):
            for c in range(3):
                pieces.append(
                    jnp.concatenate(
                        [
                            planes[c, 2 * xp + jj + dj, pl.ds(b, count_y)].reshape(rows, LANES)
                            for xp in range(count_x // 2)
                        ],
                        axis=0,
                    )
                )
        for half in range(3):
            both = jnp.concatenate([pieces[2 * half], pieces[2 * half + 1]], axis=1)
            prod = jnp.dot(turned[...], both, preferred_element_type=F32)
            for s in range(2):
                dj, c = divmod(2 * half + s, 3)
                for p in range(2):
                    a = jj + dj - p
                    val = prod[p * LANES : (p + 1) * LANES, s * LANES : (s + 1) * LANES]
                    slot = (a + 1) * 9 + 3 * b + c
                    out[slot] += val
        return carry

    lax.fori_loop(0, 6, body, 0)


def enter_kernel(in_ref, slots_ref, cot_ref, x_ref, g_ref, mask_ref, scratch):
    depth = x_ref.shape[2]
    slots, width = cot_ref.shape
    count = in_ref.shape[0]
    hot = (slots_ref[...] == iota((slots, count), 0)).astype(F32)
    active = jnp.sum(hot, axis=1, keepdims=True)
    rows = jnp.dot(
        hot.astype(BF16), in_ref[:, :width], preferred_element_type=F32
    ).astype(BF16)
    spread_columns(rows, scratch, None, depth)
    x_ref[...] = scratch[...].astype(BF16).reshape(x_ref.shape)
    masked = (cot_ref[...].astype(F32) * active).astype(BF16)
    spread_columns(masked, scratch, None, depth)
    g_ref[...] = scratch[...].astype(BF16).reshape(g_ref.shape)
    wide = jnp.broadcast_to(active, (slots, LANES))
    for z in range(depth):
        scratch[pl.ds(z, slots, stride=depth), :] = wide
    mask_ref[...] = scratch[...].astype(BF16).reshape(mask_ref.shape)


def middle_kernel(
    xh_ref, gh_ref, mask_ref, w1_ref, w2_ref,
    act_ref, hg_ref, dw1_ref, dw2_ref,
    x3, g3, t1, t2, turned,
):
    count_x, count_y, depth, _ = act_ref.shape
    rows = count_y * depth
    shift_planes(xh_ref, x3)
    shift_planes(gh_ref, g3)
    pair_weights(w1_ref, t1, True)
    pair_weights(w2_ref, t2, False)

    def body(xp, carry):
        hidden2 = pair_conv(x3, t1, xp, count_y)
        grad2 = pair_conv(g3, t2, xp, count_y)
        for p in range(2):
            x = 2 * xp + p
            mask = mask_ref[x].reshape(rows, LANES).astype(F32)
            hidden = mask * hidden2[:, p * LANES : (p + 1) * LANES]
            grad = grad2[:, p * LANES : (p + 1) * LANES]
            s = 1.0 / (1.0 + jnp.exp(-hidden))
            act_ref[x] = (hidden * s).astype(BF16).reshape(count_y, depth, LANES)
            hg = mask * grad * s * (1.0 + hidden * (1.0 - s))
            hg_ref[x] = hg.astype(BF16).reshape(count_y, depth, LANES)
        return carry

    lax.fori_loop(0, count_x // 2, body, 0)
    correlate(hg_ref, x3, turned, dw1_ref, False)
    correlate(act_ref, g3, turned, dw2_ref, True)


def leave_kernel(
    ah_ref, hh_ref, x_ref, g_ref, mask_ref, slots_ref, w1_ref, w2_ref,
    out_ref, back_ref,
    a3, h3, t1, t2, s_out, s_grad,
):
    count_x, count_y, depth, _ = x_ref.shape
    rows = count_y * depth
    slots, width = out_ref.shape
    shift_planes(ah_ref, a3)
    shift_planes(hh_ref, h3)
    pair_weights(w2_ref, t2, True)
    pair_weights(w1_ref, t1, False)

    def body(xp, carry):
        second2 = pair_conv(a3, t2, xp, count_y)
        grad2 = pair_conv(h3, t1, xp, count_y)
        for p in range(2):
            x = 2 * xp + p
            at = pl.ds(pl.multiple_of(x * rows, rows), rows)
            mask = mask_ref[x].reshape(rows, LANES).astype(F32)
            own = x_ref[x].reshape(rows, LANES).astype(F32)
            cot = g_ref[x].reshape(rows, LANES).astype(F32)
            s_out[at, :] = own + mask * second2[:, p * LANES : (p + 1) * LANES]
            s_grad[at, :] = cot + grad2[:, p * LANES : (p + 1) * LANES]
        return carry

    lax.fori_loop(0, count_x // 2, body, 0)
    out_ref[...] = gather_columns(s_out, slots, depth, width)
    grads = gather_columns(s_grad, slots, depth, width)
    count = slots_ref.shape[0]
    hot = (slots_ref[...] == iota((count, slots), 1)).astype(F32).astype(BF16)
    back_ref[...] = jnp.dot(hot, grads, preferred_element_type=F32).astype(BF16)


def extended(block, sides, width):
    for axis, dim in sides:
        count = lax.axis_size(axis)
        forward = [(i, i + 1) for i in range(count - 1)]
        backward = [(target, source) for source, target in forward]
        low = lax.ppermute(
            lax.slice_in_dim(block, block.shape[dim] - width, None, axis=dim), axis, forward
        )
        high = lax.ppermute(lax.slice_in_dim(block, 0, width, axis=dim), axis, backward)
        block = jnp.concatenate([low, block, high], axis=dim)
    return block


def on_device(column_features, column_route, cotangent, first_weight, second_weight):
    count_x = lax.axis_size("rx")
    count_y = lax.axis_size("ry")
    count_all = count_x * count_y
    shard_rows, row_width = column_features.shape
    region_x, region_y = cotangent.shape[:2]
    channels = first_weight.shape[1]
    depth = row_width // channels
    region_slots = region_x * region_y
    capacity = 2 * shard_rows // count_all
    capacity_all = count_all * capacity
    owners = column_route // region_slots
    slot_ids = column_route % region_slots
    shard_index = jnp.arange(shard_rows, dtype=jnp.int32)
    earlier = shard_index[:, None] > shard_index[None, :]
    same_owner = owners[:, None] == owners[None, :]
    ranks = jnp.sum(jnp.logical_and(earlier, same_owner).astype(jnp.int32), axis=1)
    send_pos = owners * capacity + ranks
    buffer_index = jnp.arange(capacity_all, dtype=jnp.int32)
    send_hot = send_pos[:, None] == buffer_index[None, :]
    send_table = send_hot.astype(BF16)
    outgoing = jnp.einsum(
        "sr,sw->rw", send_table, column_features, preferred_element_type=F32
    ).astype(BF16)
    filled = jnp.sum(send_hot.astype(jnp.int32), axis=0)
    slot_total = jnp.sum(jnp.where(send_hot, slot_ids[:, None], 0), axis=0)
    out_slots = jnp.where(filled > 0, slot_total, region_slots).astype(BF16)
    outgoing = jnp.concatenate(
        [outgoing, jnp.broadcast_to(out_slots[:, None], (capacity_all, LANES))], axis=1
    )
    incoming = lax.all_to_all(
        outgoing.reshape(count_all, capacity, row_width + LANES),
        ("rx", "ry"),
        split_axis=0,
        concat_axis=0,
        tiled=True,
    ).reshape(capacity_all, row_width + LANES)
    in_slots = incoming[:, row_width].astype(jnp.int32)

    cot_rows = cotangent.reshape(region_slots, row_width)
    field = jax.ShapeDtypeStruct((region_x, region_y, depth, LANES), BF16)
    planes = pltpu.VMEM((3, region_x + 2, region_y + 2, depth, LANES), BF16)
    table = pltpu.VMEM((36 * LANES, 2 * LANES), BF16)
    voxels = region_slots * depth
    grad_shape = jax.ShapeDtypeStruct((45, LANES, LANES), F32)
    x_own, g_own, mask = pl.pallas_call(
        enter_kernel,
        out_shape=(field, field, field),
        scratch_shapes=[pltpu.VMEM((voxels, LANES), F32)],
        compiler_params=params(),
    )(incoming, in_slots[None, :], cot_rows)
    sides = (("rx", 0), ("ry", 1))
    xh = extended(x_own, sides, 1)
    gh = extended(g_own, sides, 1)
    act, hg, dw1, dw2 = pl.pallas_call(
        middle_kernel,
        out_shape=(field, field, grad_shape, grad_shape),
        scratch_shapes=[planes, planes, table, table, pltpu.VMEM((2 * LANES, voxels // 2), BF16)],
        compiler_params=params(),
    )(xh, gh, mask, first_weight, second_weight)
    ah = extended(act, sides, 1)
    hh = extended(hg, sides, 1)
    out_rows, back_rows = pl.pallas_call(
        leave_kernel,
        out_shape=(
            jax.ShapeDtypeStruct((region_slots, row_width), BF16),
            jax.ShapeDtypeStruct((capacity_all, row_width), BF16),
        ),
        scratch_shapes=[
            planes, planes, table, table,
            pltpu.VMEM((voxels, LANES), F32), pltpu.VMEM((voxels, LANES), F32),
        ],
        compiler_params=params(),
    )(ah, hh, x_own, g_own, mask, in_slots[:, None], first_weight, second_weight)
    returned = lax.all_to_all(
        back_rows.reshape(count_all, capacity, row_width),
        ("rx", "ry"),
        split_axis=0,
        concat_axis=0,
        tiled=True,
    ).reshape(capacity_all, row_width)
    feature_grads = jnp.dot(send_table, returned, preferred_element_type=F32).astype(BF16)

    first_local = dw1[9:36, :channels, :channels]
    second_local = jnp.transpose(dw2[9:36, :channels, :channels][::-1], (0, 2, 1))
    both = jnp.stack([first_local, second_local]).astype(BF16).reshape(count_all, -1)
    spread = lax.all_to_all(both, ("rx", "ry"), split_axis=0, concat_axis=0, tiled=True)
    share = jnp.sum(spread.astype(F32), axis=0).astype(BF16)
    whole = lax.all_gather(share, ("rx", "ry"), axis=0, tiled=True)
    factor = 1.0 / jnp.sqrt(F32(count_all * shard_rows * depth))
    scaled = (whole.astype(F32) * factor).reshape(2, 27, channels, channels)
    return (
        out_rows.reshape(region_x, region_y, row_width),
        feature_grads,
        scaled[0],
        scaled[1],
    )


def solution(mesh):
    in_specs = (P(("rx", "ry"), None), P(("rx", "ry")), P("rx", "ry", None), P(), P())
    out_specs = (P("rx", "ry", None), P(("rx", "ry"), None), P(), P())
    return jax.shard_map(
        on_device, mesh=mesh, in_specs=in_specs, out_specs=out_specs, check_vma=False
    )
```

time: 677 us -> 386 us (0.57)
  matrix products: 336 us -> 1.53 us
  local copies, waits for them, and re-layouts: 101 us -> 32.6 us
  Pallas kernels: 0 us -> 63 us
  blocking collectives: 0 us -> 28.4 us
  waiting for transfers between devices: 131 us -> 152 us
  starting transfers between devices: 76.5 us -> 68.5 us
  other arithmetic: 10.5 us -> 18.2 us
    dot_general x165 -> x1, matrix products: 335 us -> 1.06 us  [on_device(): jnp.dot(send_table, returned, preferred_element_type=F32).astype(BF16)]
    unnamed x1 -> x2, waiting for transfers between devices: 0.68 us -> 135 us
    psum x1 -> x0, waiting for transfers between devices: 121 us -> none  [on_device(): lax.psum((first_local, second_local), ('rx', 'ry'))]
    pallas_call x0 -> x3, Pallas kernels: none -> 63 us  [the longest x1 31.8 us: on_device(): pl.pallas_call(middle_kernel, out_shape=(field, field, grad_shape, grad_s...]
    reshape x16 -> x4, local copies, waits for them, and re-layouts: 53.8 us -> 5.75 us  [the longest x1 2.84 us: on_device(): back_rows.reshape(count_all, capacity, row_width)]
    all_to_all x0 -> x1, blocking collectives: none -> 28.4 us  [on_device(): lax.all_to_all(outgoing.reshape(count_all, capacity, row_width + LANES),...]
    convert_element_type x4 -> x2, local copies, waits for them, and re-layouts: 27.2 us -> 6.41 us  [on_device(): jnp.stack([first_local, second_local]).astype(BF16).reshape(count_all, -1)]
    all_to_all x3 -> x2, waiting for transfers between devices: 0.01 us -> 11.2 us  [the longest x1 11.2 us: on_device(): lax.all_to_all(back_rows.reshape(count_all, capacity, row_width), ('rx',...]
  transfers between devices with their start and end apart: 20 -> 19, of which waited for: 5 -> 5; matrix products, arithmetic and copies ran while one was open for 32% -> 5% of each run, Pallas kernels for 0% -> 6%
where the time goes in v1:
time: 386 us; the launch traced here: 379 us
  waiting for transfers between devices  152 us (39%)
  starting transfers between devices  68.5 us (18%)
  Pallas kernels  63 us (16%)
  local copies, waits for them, and re-layouts  32.6 us (8%)
  blocking collectives  28.4 us (7%)
  other arithmetic  18.2 us (5%)
  between operations  14.8 us (4%)
    unnamed x2, waiting for transfers between devices  135 us
    pallas_call x1, Pallas kernels, on_device(): pl.pallas_call(middle_kernel, out_shape=(field, field, grad_shape, grad_s...  31.8 us
    all_to_all x1, blocking collectives, on_device(): lax.all_to_all(outgoing.reshape(count_all, capacity, row_width + LANES),...  28.4 us
    ppermute x8, starting transfers between devices, extended(): lax.ppermute(lax.slice_in_dim(block, block.shape[dim] - width, None, axis...  27.7 us
    pallas_call x1, Pallas kernels, on_device(): pl.pallas_call(leave_kernel, out_shape=(jax.ShapeDtypeStruct((region_slot...  22.3 us
    all_to_all x1, starting transfers between devices, on_device(): lax.all_to_all(back_rows.reshape(count_all, capacity, row_width), ('rx',...  15.7 us
    ppermute x8, starting transfers between devices, extended(): lax.ppermute(lax.slice_in_dim(block, 0, width, axis=dim), axis, backward)  13.1 us
    all_to_all x1, starting transfers between devices, on_device(): lax.all_to_all(both, ('rx', 'ry'), split_axis=0, concat_axis=0, tiled=True)  12 us
  transfers between devices with their start and end apart: 19, of which 5 were waited for; matrix products, arithmetic and copies ran while one was open for 5% of the time, Pallas kernels for 6%

profile of v1, /device:TPU:1, one launch (start us, length us, event | category | flops | bytes accessed | tf_op | source)
XLA Modules:
  0.0 378.8 jit_solution(15380874647166471899)
XLA Ops:
  9.2 28.4 %all_to_all.16 = bf16[128,2,1664]{2,1,0:T(2,128)(2,1)S(1)} all-to-all(bf16[128,2,1664]{2,1,0:T(2,128)(2,1)S(1)} %reshape.85), channel_id=1, replica_groups=mesh['rx'=8,'ry'=16] {'rx','ry'}, dimensions={0} | all-to-all | bytes 1703936 | tf_op jit(solution)/shard_map/all_to_all | solution.py:280
  39.4 8.9 %shard_map.84 = (bf16[16,16,16,128]{3,2,1,0:T(8,128)(2,1)}, bf16[16,16,16,128]{3,2,1,0:T(8,128)(2,1)}, bf16[16,16,16,128]{3,2,1,0:T(8,128)(2,1)}) custom-call(bf16[256,1664]{1,0:T(8,128)(2,1)} %copy-done.3, s32[1,256]{1,0:T(1,128)} %bitcast.14, bf16[256,1536]{1,0:T(8,128)(2,1)} %bitcast.13), custom_call_target="tpu_custom_call" | custom-call | tf_op jit(solution)/shard_map/pallas_call | solution.py:295
  49.2 3.2 collective-permute-start.4
  52.3 1.9 collective-permute-start.5
  55.2 3.6 collective-permute-start
  58.8 1.9 collective-permute-start.1
  60.8 1.6 constant_dynamic-update-slice_fusion.4
  62.4 2.5 collective-permute-start.6
  66.6 4.0 %collective-permute-start.2 = (bf16[18,1,16,128]{3,2,1,0:T(8,128)(2,1)S(1)}, bf16[18,1,16,128]{3,2,1,0:T(8,128)(2,1)S(1)}, u32[]{:S(2)}, u32[]{:S(2)}) collective-permute-start(bf16[18,1,16,128]{3,2,1,0:T(8,128)(2,1)S(1)} %get-tuple-element.32), channel_id=1, source_target_pairs={{0,1},{1,2},{2,3},{3,4},{4,5},{5,6},{6,7},{7,8},{8,9},{9,10},{10,1... | collective-permute-start | bytes 221192 | tf_op jit(solution)/shard_map/ppermute | solution.py:242
  70.5 1.6 collective-permute-start.3
  73.4 2.5 collective-permute-done.3
  77.1 31.8 %shard_map.85 = (bf16[16,16,16,128]{3,2,1,0:T(8,128)(2,1)}, bf16[16,16,16,128]{3,2,1,0:T(8,128)(2,1)}, f32[45,128,128]{2,1,0:T(8,128)}, f32[45,128,128]{2,1,0:T(8,128)}) custom-call(bf16[18,18,16,128]{3,2,1,0:T(8,128)(2,1)} %pad_maximum_fusion.xh_ref, bf16[18,18,16,128]{3,2,1,0:T(8,128)(2,1)} %pad_maximum_fusion.1.gh_ref, ...), custom_call_target="tpu_custom_call" | custom-call | tf_op jit(solution)/shard_map/pallas_call | solution.py:304
  108.9 2.7 copy.15
  114.9 5.9 %convert_element_type.64 = bf16[128,1,3888]{2,1,0:T(2,128)(2,1)S(1)} reshape(bf16[2,27,96,96]{3,2,1,0:T(8,128)(2,1)} %copy.16) | data formatting | bytes 1990656 | tf_op jit(solution)/shard_map/convert_element_type | solution.py:335
  121.3 7.1 %reduce.4 = bf16[128,3888]{1,0:T(8,128)(2,1)S(1)} reduce(bf16[128,1,3888]{2,1,0:T(2,128)(2,1)S(1)} %convert_element_type.64, bf16[]{:T(256)} %broadcast.38), dimensions={1}, to_apply=%convert_element_type.64.reduce_sub_computation | reduce | bytes 1990658 | tf_op jit(solution)/shard_map/convert_element_type | solution.py:335
  128.4 2.4 reshape.95
  130.8 12.0 %all-to-all-start.2 = ((bf16[128,2,1944]{2,1,0:T(2,128)(2,1)}), bf16[128,2,1944]{2,1,0:T(2,128)(2,1)S(1)}, u32[]{:S(2)}, u32[]{:S(2)}) async-start(bf16[128,2,1944]{2,1,0:T(2,128)(2,1)} %reshape.95), calls=%async_computation.2 | async-start | bytes 2097152 | tf_op jit(solution)/shard_map/all_to_all | solution.py:336
  143.6 3.5 collective-permute-start.12
  147.2 1.9 collective-permute-start.13
  149.1 3.6 collective-permute-start.8
  152.8 1.9 collective-permute-start.9
  156.7 3.2 collective-permute-start.14
  161.5 4.0 %collective-permute-start.10 = (bf16[18,1,16,128]{3,2,1,0:T(8,128)(2,1)S(1)}, bf16[18,1,16,128]{3,2,1,0:T(8,128)(2,1)S(1)}, u32[]{:S(2)}, u32[]{:S(2)}) collective-permute-start(bf16[18,1,16,128]{3,2,1,0:T(8,128)(2,1)S(1)} %get-tuple-element.28), channel_id=1, source_target_pairs={{0,1},{1,2},{2,3},{3,4},{4,5},{5,6},{6,7},{7,8},{8,9},{9,10},{10,1... | collective-permute-start | bytes 221192 | tf_op jit(solution)/shard_map/ppermute | solution.py:242
  168.1 2.5 collective-permute-done.11
  171.9 22.3 %shard_map.86 = (bf16[256,1536]{1,0:T(8,128)(2,1)}, bf16[256,1536]{1,0:T(8,128)(2,1)}) custom-call(bf16[18,18,16,128]{3,2,1,0:T(8,128)(2,1)} %pad_maximum_fusion.2.ah_ref, bf16[18,18,16,128]{3,2,1,0:T(8,128)(2,1)} %pad_maximum_fusion.3.hh_ref, bf16[16,16,16,128]{3,2,1,0:T(8,128)(2,1)} %get-tuple-element.13.x_ref, ...), custom_call_target="tpu_custom_call" | custom-call | tf_op jit(solution)/shard_map/pallas_call | solution.py:312
  194.2 2.8 reshape.89
  197.1 15.7 %all-to-all-start.1 = ((bf16[128,2,1536]{2,1,0:T(2,128)(2,1)}), bf16[128,2,1536]{2,1,0:T(2,128)(2,1)}, u32[]{:S(2)}, u32[]{:S(2)}) async-start(bf16[128,2,1536]{2,1,0:T(2,128)(2,1)} %reshape.89), calls=%async_computation.1 | async-start | bytes 1572864 | tf_op jit(solution)/shard_map/all_to_all | solution.py:324
  212.8 1.6 reshape.96
  214.4 2.0 reduce_sum.42
  217.7 11.2 %all-to-all-done.1 = bf16[128,2,1536]{2,1,0:T(2,128)(2,1)} async-done(((bf16[128,2,1536]{2,1,0:T(2,128)(2,1)}), bf16[128,2,1536]{2,1,0:T(2,128)(2,1)}, u32[]{:S(2)}, u32[]{:S(2)}) %all-to-all-start.1) | async-done | bytes 786464 | tf_op jit(solution)/shard_map/all_to_all | solution.py:324
  228.9 2.3 reshape.90
  232.2 135.2 %all-reduce.3.cloned.1.call-done = bf16[497664]{0:T(1024)(128)(2,1)} async-done(((bf16[497664]{0:T(1024)(128)(2,1)}), bf16[497664]{0:T(1024)(128)(2,1)}) %all-reduce.3.cloned.1.call-update) | async-done | bytes 995344
  (78 shorter events, 28.3 us)
Async XLA Ops:
  7.2 1.0 copy-start
  37.9 1.5 copy-start.3
  49.2 11.6 %collective-permute-start.4 = (bf16[1,16,16,128]{3,2,1,0:T(8,128)(2,1)S(1)}, bf16[1,16,16,128]{3,2,1,0:T(8,128)(2,1)S(1)}, u32[]{:S(2)}, u32[]{:S(2)}) collective-permute-start(bf16[1,16,16,128]{3,2,1,0:T(8,128)(2,1)S(1)} %get-tuple-element.39), channel_id=1, source_target_pairs={{0,16},{16,32},{32,48},{48,64},{64,80},{80,96},{96,112},{1,17},{17... | collective-permute-start | bytes 196616 | tf_op jit(solution)/shard_map/ppermute | solution.py:242
  52.3 10.0 %collective-permute-start.5 = (bf16[1,16,16,128]{3,2,1,0:T(8,128)(2,1)S(1)}, bf16[1,16,16,128]{3,2,1,0:T(8,128)(2,1)S(1)}, u32[]{:S(2)}, u32[]{:S(2)}) collective-permute-start(bf16[1,16,16,128]{3,2,1,0:T(8,128)(2,1)S(1)} %get-tuple-element.38), channel_id=1, source_target_pairs={{16,0},{32,16},{48,32},{64,48},{80,64},{96,80},{112,96},{17,1},{33... | collective-permute-start | bytes 196616 | tf_op jit(solution)/shard_map/ppermute | solution.py:245
  55.2 11.1 %collective-permute-start = (bf16[1,16,16,128]{3,2,1,0:T(8,128)(2,1)S(1)}, bf16[1,16,16,128]{3,2,1,0:T(8,128)(2,1)S(1)}, u32[]{:S(2)}, u32[]{:S(2)}) collective-permute-start(bf16[1,16,16,128]{3,2,1,0:T(8,128)(2,1)S(1)} %get-tuple-element.41), channel_id=1, source_target_pairs={{0,16},{16,32},{32,48},{48,64},{64,80},{80,96},{96,112},{1,17},{17... | collective-permute-start | bytes 196616 | tf_op jit(solution)/shard_map/ppermute | solution.py:242
  58.8 7.7 %collective-permute-start.1 = (bf16[1,16,16,128]{3,2,1,0:T(8,128)(2,1)S(1)}, bf16[1,16,16,128]{3,2,1,0:T(8,128)(2,1)S(1)}, u32[]{:S(2)}, u32[]{:S(2)}) collective-permute-start(bf16[1,16,16,128]{3,2,1,0:T(8,128)(2,1)S(1)} %get-tuple-element.40), channel_id=1, source_target_pairs={{16,0},{32,16},{48,32},{64,48},{80,64},{96,80},{112,96},{17,1},{33... | collective-permute-start | bytes 196616 | tf_op jit(solution)/shard_map/ppermute | solution.py:245
  60.8 5.5 %copy-start.1 = (bf16[16,16,16,128]{3,2,1,0:T(8,128)(2,1)S(1)}, bf16[16,16,16,128]{3,2,1,0:T(8,128)(2,1)}, u32[]{:S(2)}) copy-start(bf16[16,16,16,128]{3,2,1,0:T(8,128)(2,1)} %get-tuple-element.13.x_ref) | copy-start | bytes 3145732
  62.4 9.7 %collective-permute-start.6 = (bf16[18,1,16,128]{3,2,1,0:T(8,128)(2,1)S(1)}, bf16[18,1,16,128]{3,2,1,0:T(8,128)(2,1)S(1)}, u32[]{:S(2)}, u32[]{:S(2)}) collective-permute-start(bf16[18,1,16,128]{3,2,1,0:T(8,128)(2,1)S(1)} %get-tuple-element.30), channel_id=1, source_target_pairs={{0,1},{1,2},{2,3},{3,4},{4,5},{5,6},{6,7},{7,8},{8,9},{9,10},{10,1... | collective-permute-start | bytes 221192 | tf_op jit(solution)/shard_map/ppermute | solution.py:242
  64.9 7.2 %collective-permute-start.7 = (bf16[18,1,16,128]{3,2,1,0:T(8,128)(2,1)S(1)}, bf16[18,1,16,128]{3,2,1,0:T(8,128)(2,1)S(1)}, u32[]{:S(2)}, u32[]{:S(2)}) collective-permute-start(bf16[18,1,16,128]{3,2,1,0:T(8,128)(2,1)S(1)} %get-tuple-element.31), channel_id=1, source_target_pairs={{1,0},{2,1},{3,2},{4,3},{5,4},{6,5},{7,6},{8,7},{9,8},{10,9},{11,1... | collective-permute-start | bytes 221192 | tf_op jit(solution)/shard_map/ppermute | solution.py:245
  66.6 6.8 %collective-permute-start.2 = (bf16[18,1,16,128]{3,2,1,0:T(8,128)(2,1)S(1)}, bf16[18,1,16,128]{3,2,1,0:T(8,128)(2,1)S(1)}, u32[]{:S(2)}, u32[]{:S(2)}) collective-permute-start(bf16[18,1,16,128]{3,2,1,0:T(8,128)(2,1)S(1)} %get-tuple-element.32), channel_id=1, source_target_pairs={{0,1},{1,2},{2,3},{3,4},{4,5},{5,6},{6,7},{7,8},{8,9},{9,10},{10,1... | collective-permute-start | bytes 221192 | tf_op jit(solution)/shard_map/ppermute | solution.py:242
  70.5 5.3 %collective-permute-start.3 = (bf16[18,1,16,128]{3,2,1,0:T(8,128)(2,1)S(1)}, bf16[18,1,16,128]{3,2,1,0:T(8,128)(2,1)S(1)}, u32[]{:S(2)}, u32[]{:S(2)}) collective-permute-start(bf16[18,1,16,128]{3,2,1,0:T(8,128)(2,1)S(1)} %get-tuple-element.33), channel_id=1, source_target_pairs={{1,0},{2,1},{3,2},{4,3},{5,4},{6,5},{7,6},{8,7},{9,8},{10,9},{11,1... | collective-permute-start | bytes 221192 | tf_op jit(solution)/shard_map/ppermute | solution.py:245
  130.8 18.4 %copy-start.4 = (bf16[16,16,16,128]{3,2,1,0:T(8,128)(2,1)S(1)}, bf16[16,16,16,128]{3,2,1,0:T(8,128)(2,1)}, u32[]{:S(2)}) copy-start(bf16[16,16,16,128]{3,2,1,0:T(8,128)(2,1)} %get-tuple-element.16) | copy-start | bytes 3145732
  130.8 66.3 %all-to-all-start.2 = ((bf16[128,2,1944]{2,1,0:T(2,128)(2,1)}), bf16[128,2,1944]{2,1,0:T(2,128)(2,1)S(1)}, u32[]{:S(2)}, u32[]{:S(2)}) async-start(bf16[128,2,1944]{2,1,0:T(2,128)(2,1)} %reshape.95), calls=%async_computation.2 | async-start | bytes 2097152 | tf_op jit(solution)/shard_map/all_to_all | solution.py:336
  143.6 11.1 %collective-permute-start.12 = (bf16[1,16,16,128]{3,2,1,0:T(8,128)(2,1)S(1)}, bf16[1,16,16,128]{3,2,1,0:T(8,128)(2,1)S(1)}, u32[]{:S(2)}, u32[]{:S(2)}) collective-permute-start(bf16[1,16,16,128]{3,2,1,0:T(8,128)(2,1)S(1)} %get-tuple-element.35), channel_id=1, source_target_pairs={{0,16},{16,32},{32,48},{48,64},{64,80},{80,96},{96,112},{1,17},{17... | collective-permute-start | bytes 196616 | tf_op jit(solution)/shard_map/ppermute | solution.py:242
  147.2 9.5 %collective-permute-start.13 = (bf16[1,16,16,128]{3,2,1,0:T(8,128)(2,1)S(1)}, bf16[1,16,16,128]{3,2,1,0:T(8,128)(2,1)S(1)}, u32[]{:S(2)}, u32[]{:S(2)}) collective-permute-start(bf16[1,16,16,128]{3,2,1,0:T(8,128)(2,1)S(1)} %get-tuple-element.34), channel_id=1, source_target_pairs={{16,0},{32,16},{48,32},{64,48},{80,64},{96,80},{112,96},{17,1},{33... | collective-permute-start | bytes 196616 | tf_op jit(solution)/shard_map/ppermute | solution.py:245
  149.1 12.1 %collective-permute-start.8 = (bf16[1,16,16,128]{3,2,1,0:T(8,128)(2,1)S(1)}, bf16[1,16,16,128]{3,2,1,0:T(8,128)(2,1)S(1)}, u32[]{:S(2)}, u32[]{:S(2)}) collective-permute-start(bf16[1,16,16,128]{3,2,1,0:T(8,128)(2,1)S(1)} %get-tuple-element.37), channel_id=1, source_target_pairs={{0,16},{16,32},{32,48},{48,64},{64,80},{80,96},{96,112},{1,17},{17... | collective-permute-start | bytes 196616 | tf_op jit(solution)/shard_map/ppermute | solution.py:242
  152.8 8.7 %collective-permute-start.9 = (bf16[1,16,16,128]{3,2,1,0:T(8,128)(2,1)S(1)}, bf16[1,16,16,128]{3,2,1,0:T(8,128)(2,1)S(1)}, u32[]{:S(2)}, u32[]{:S(2)}) collective-permute-start(bf16[1,16,16,128]{3,2,1,0:T(8,128)(2,1)S(1)} %get-tuple-element.36), channel_id=1, source_target_pairs={{16,0},{32,16},{48,32},{64,48},{80,64},{96,80},{112,96},{17,1},{33... | collective-permute-start | bytes 196616 | tf_op jit(solution)/shard_map/ppermute | solution.py:245
  156.7 10.2 %collective-permute-start.14 = (bf16[18,1,16,128]{3,2,1,0:T(8,128)(2,1)S(1)}, bf16[18,1,16,128]{3,2,1,0:T(8,128)(2,1)S(1)}, u32[]{:S(2)}, u32[]{:S(2)}) collective-permute-start(bf16[18,1,16,128]{3,2,1,0:T(8,128)(2,1)S(1)} %get-tuple-element.26), channel_id=1, source_target_pairs={{0,1},{1,2},{2,3},{3,4},{4,5},{5,6},{6,7},{7,8},{8,9},{9,10},{10,1... | collective-permute-start | bytes 221192 | tf_op jit(solution)/shard_map/ppermute | solution.py:242
  159.9 6.9 %collective-permute-start.15 = (bf16[18,1,16,128]{3,2,1,0:T(8,128)(2,1)S(1)}, bf16[18,1,16,128]{3,2,1,0:T(8,128)(2,1)S(1)}, u32[]{:S(2)}, u32[]{:S(2)}) collective-permute-start(bf16[18,1,16,128]{3,2,1,0:T(8,128)(2,1)S(1)} %get-tuple-element.27), channel_id=1, source_target_pairs={{1,0},{2,1},{3,2},{4,3},{5,4},{6,5},{7,6},{8,7},{9,8},{10,9},{11,1... | collective-permute-start | bytes 221192 | tf_op jit(solution)/shard_map/ppermute | solution.py:245
  161.5 6.6 %collective-permute-start.10 = (bf16[18,1,16,128]{3,2,1,0:T(8,128)(2,1)S(1)}, bf16[18,1,16,128]{3,2,1,0:T(8,128)(2,1)S(1)}, u32[]{:S(2)}, u32[]{:S(2)}) collective-permute-start(bf16[18,1,16,128]{3,2,1,0:T(8,128)(2,1)S(1)} %get-tuple-element.28), channel_id=1, source_target_pairs={{0,1},{1,2},{2,3},{3,4},{4,5},{5,6},{6,7},{7,8},{8,9},{9,10},{10,1... | collective-permute-start | bytes 221192 | tf_op jit(solution)/shard_map/ppermute | solution.py:242
  165.5 5.1 %collective-permute-start.11 = (bf16[18,1,16,128]{3,2,1,0:T(8,128)(2,1)S(1)}, bf16[18,1,16,128]{3,2,1,0:T(8,128)(2,1)S(1)}, u32[]{:S(2)}, u32[]{:S(2)}) collective-permute-start(bf16[18,1,16,128]{3,2,1,0:T(8,128)(2,1)S(1)} %get-tuple-element.29), channel_id=1, source_target_pairs={{1,0},{2,1},{3,2},{4,3},{5,4},{6,5},{7,6},{8,7},{9,8},{10,9},{11,1... | collective-permute-start | bytes 221192 | tf_op jit(solution)/shard_map/ppermute | solution.py:245
  197.1 31.8 %all-to-all-start.1 = ((bf16[128,2,1536]{2,1,0:T(2,128)(2,1)}), bf16[128,2,1536]{2,1,0:T(2,128)(2,1)}, u32[]{:S(2)}, u32[]{:S(2)}) async-start(bf16[128,2,1536]{2,1,0:T(2,128)(2,1)} %reshape.89), calls=%async_computation.1 | async-start | bytes 1572864 | tf_op jit(solution)/shard_map/all_to_all | solution.py:324
  212.7 154.7 %all-reduce.3.cloned.1.call-start = ((), (), s32[]{:S(2)}) async-start(), calls=%async_computation.3 | async-start | bytes 1990656
  216.7 0.9 copy-start.2
Sparse Core Ops, SparseCore 0:
  218.9 148.4 all-reduce.2

commit v2 on v1

v2 whole, which is shorter than its diff:
```python
import functools

import jax
import jax.numpy as jnp
from jax import lax
from jax.experimental import pallas as pl
from jax.experimental.pallas import tpu as pltpu
from jax.sharding import PartitionSpec as P

F32 = jnp.float32
BF16 = jnp.bfloat16
LANES = 128
VMEM_LIMIT = 64 * 1024 * 1024 - 64 * 1024
SIDES = [(dx, dy) for dx in (-1, 0, 1) for dy in (-1, 0, 1) if (dx, dy) != (0, 0)]


def params():
    return pltpu.CompilerParams(vmem_limit_bytes=VMEM_LIMIT)


def iota(shape, dim):
    return lax.broadcasted_iota(jnp.int32, shape, dim)


def build_move(move, depth):
    width = move.shape[0]
    k = iota((width, 2 * LANES), 0)
    n = iota((width, 2 * LANES), 1)
    base = k - (n % LANES) * depth - n // LANES
    for zp in range(depth // 2):
        move[:, zp * 2 * LANES : (zp + 1) * 2 * LANES] = jnp.where(
            base == 2 * zp, 1.0, 0.0
        ).astype(BF16)


def spread_columns(rows, scale, move, scratch, depth):
    count = rows.shape[0]
    for zp in range(depth // 2):
        moved = jnp.dot(
            rows, move[:, zp * 2 * LANES : (zp + 1) * 2 * LANES], preferred_element_type=F32
        )
        if scale is not None:
            moved = moved * scale
        scratch[pl.ds(2 * zp, count, stride=depth), :] = moved[:, :LANES]
        scratch[pl.ds(2 * zp + 1, count, stride=depth), :] = moved[:, LANES:]


def gather_columns(scratch, move, count, depth):
    wide = jnp.concatenate(
        [scratch[pl.ds(z, count, stride=depth), :] for z in range(depth)], axis=1
    ).astype(BF16)
    return lax.dot_general(
        wide, move[...], (((1,), (1,)), ((), ())), preferred_element_type=F32
    ).astype(BF16)


def shift_block(planes, xs, ys):
    block = planes[1, xs, ys]
    count_x, count_y, depth, lanes = block.shape
    total = count_x * count_y * depth
    z = iota((total, lanes), 0) % depth
    v = block.astype(F32).reshape(total, lanes)
    below = jnp.where(z == 0, 0.0, pltpu.roll(v, 1, 0))
    above = jnp.where(z == depth - 1, 0.0, pltpu.roll(v, total - 1, 0))
    planes[0, xs, ys] = below.astype(BF16).reshape(block.shape)
    planes[2, xs, ys] = above.astype(BF16).reshape(block.shape)


def shift_inside(planes):
    rows, columns = planes.shape[1] - 2, planes.shape[2] - 2

    def body(x, carry):
        shift_block(planes, pl.ds(x + 1, 1), pl.ds(1, columns))
        return carry

    lax.fori_loop(0, rows, body, 0)


def shift_border(planes):
    rows, columns = planes.shape[1] - 2, planes.shape[2] - 2
    shift_block(planes, pl.ds(0, 1), pl.ds(0, columns + 2))
    shift_block(planes, pl.ds(rows + 1, 1), pl.ds(0, columns + 2))
    shift_block(planes, pl.ds(1, rows), pl.ds(0, 1))
    shift_block(planes, pl.ds(1, rows), pl.ds(columns + 1, 1))


def clear_border(planes):
    _, count_x, count_y, depth, lanes = planes.shape
    planes[1, 0] = jnp.zeros((count_y, depth, lanes), BF16)
    planes[1, count_x - 1] = jnp.zeros((count_y, depth, lanes), BF16)
    planes[1, :, 0] = jnp.zeros((count_x, depth, lanes), BF16)
    planes[1, :, count_y - 1] = jnp.zeros((count_x, depth, lanes), BF16)


def pair_weights(weights, table, transposed):
    channels = weights.shape[1]
    table[...] = jnp.zeros(table.shape, BF16)
    for a in range(3):
        for b in range(3):
            for c in range(3):
                tap = 9 * a + 3 * b + c
                if transposed:
                    block = weights[tap].astype(F32).T.astype(BF16)
                else:
                    block = weights[26 - tap]
                for p in range(2):
                    row = ((a + p) * 9 + 3 * b + c) * LANES
                    table[row : row + channels, p * LANES : p * LANES + channels] = block


def pair_conv(planes, table, xp, count_y):
    depth = planes.shape[3]
    pieces = []
    for j in range(4):
        for b in range(3):
            for c in range(3):
                pieces.append(
                    planes[c, 2 * xp + j, b : b + count_y].reshape(count_y * depth, LANES)
                )
    return jnp.dot(jnp.concatenate(pieces, axis=1), table[...], preferred_element_type=F32)


def correlate(local, planes, turned, out):
    _, count_x, count_y, depth, _ = local.shape
    count_x, count_y = count_x - 2, count_y - 2
    rows = count_y * depth
    for xp in range(count_x // 2):
        pair = jnp.concatenate(
            [
                local[1, 2 * xp + 1, 1 : count_y + 1].reshape(rows, LANES),
                local[1, 2 * xp + 2, 1 : count_y + 1].reshape(rows, LANES),
            ],
            axis=1,
        )
        turned[:, xp * rows : (xp + 1) * rows] = pair.astype(F32).T.astype(BF16)
    out[...] = jnp.zeros(out.shape, F32)

    def body(step, carry):
        jj = (step // 3) * 2
        b = step % 3
        pieces = []
        for dj in range(2):
            for c in range(3):
                pieces.append(
                    jnp.concatenate(
                        [
                            planes[c, 2 * xp + jj + dj, pl.ds(b, count_y)].reshape(rows, LANES)
                            for xp in range(count_x // 2)
                        ],
                        axis=0,
                    )
                )
        for half in range(3):
            both = jnp.concatenate([pieces[2 * half], pieces[2 * half + 1]], axis=1)
            prod = jnp.dot(turned[...], both, preferred_element_type=F32)
            for s in range(2):
                dj, c = divmod(2 * half + s, 3)
                for p in range(2):
                    slot = (jj + dj - p + 1) * 9 + 3 * b + c
                    out[slot] += prod[p * LANES : (p + 1) * LANES, s * LANES : (s + 1) * LANES]
        return carry

    lax.fori_loop(0, 6, body, 0)


def pack_grads(out, packed, base, flip, channels):
    tall = channels * channels // LANES
    rest = channels - tall
    lane = iota((tall, LANES), 1)

    def body(k, carry):
        block = out[9 + 26 - k].T if flip else out[9 + k]
        low = block[tall:channels]
        part = LANES - channels
        moved = jnp.concatenate(
            [pltpu.roll(low, channels - part * m, 1) for m in range(tall // rest)], axis=0
        )
        at = pl.ds(pl.multiple_of((base + k) * tall, 8), tall)
        packed[at, :] = jnp.where(lane < channels, block[:tall], moved)
        return carry

    lax.fori_loop(0, 27, body, 0)


def unpack_grads(packed, dest, base, factor, channels):
    tall = channels * channels // LANES
    rest = channels - tall
    part = LANES - channels
    lane = iota((rest, LANES), 1)

    def body(k, carry):
        v = packed[pl.ds(pl.multiple_of((base + k) * tall, 8), tall), :] * factor
        low = jnp.zeros((rest, LANES), F32)
        for m in range(tall // rest):
            turned = pltpu.roll(v[m * rest : (m + 1) * rest], (part * m - channels) % LANES, 1)
            low = jnp.where(lane // part == m, turned, low)
        dest[k, :tall, :] = v[:, :channels]
        dest[k, tall:, :] = low[:, :channels]
        return carry

    lax.fori_loop(0, 27, body, 0)


class Halo:
    def __init__(self, planes, send_sem, recv_sem, grid):
        self.planes, self.send_sem, self.recv_sem, self.grid = planes, send_sem, recv_sem, grid
        self.extent = (planes.shape[1] - 2, planes.shape[2] - 2)

    def copy(self, k):
        source, target = [], []
        for step, extent in zip(SIDES[k], self.extent):
            source.append({0: pl.ds(1, extent), 1: pl.ds(extent, 1), -1: pl.ds(1, 1)}[step])
            target.append({0: pl.ds(1, extent), 1: pl.ds(0, 1), -1: pl.ds(extent + 1, 1)}[step])
        (ix, iy, _, _), (dx, dy) = self.grid, SIDES[k]
        return pltpu.make_async_remote_copy(
            src_ref=self.planes.at[1, source[0], source[1]],
            dst_ref=self.planes.at[1, target[0], target[1]],
            send_sem=self.send_sem.at[k],
            recv_sem=self.recv_sem.at[k],
            device_id=(ix + dx, iy + dy),
            device_id_type=pl.DeviceIdType.MESH,
        )

    def there(self, dx, dy):
        ix, iy, nx, ny = self.grid
        return jnp.logical_and(
            jnp.logical_and(ix + dx >= 0, ix + dx < nx), jnp.logical_and(iy + dy >= 0, iy + dy < ny)
        )

    def start(self):
        for k, (dx, dy) in enumerate(SIDES):

            @pl.when(self.there(dx, dy))
            def _():
                self.copy(k).start()

    def wait(self):
        for k, (dx, dy) in enumerate(SIDES):

            @pl.when(self.there(-dx, -dy))
            def _():
                self.copy(k).wait_recv()

            @pl.when(self.there(dx, dy))
            def _():
                self.copy(k).wait_send()


def core_kernel(
    nx, ny, factor,
    in_ref, slot_row_ref, slot_col_ref, cot_ref, w1_ref, w2_ref,
    out_ref, back_ref, dw1_ref, dw2_ref,
    x3, g3, a3, h3, tx, tg, ta, th, move, s1, s2, mask_p, turned, grads,
    packed, shares, spread, whole,
    halo_send, halo_recv, sum_send, sum_recv,
):
    ix, iy = lax.axis_index("rx"), lax.axis_index("ry")
    count = nx * ny
    me = ix * ny + iy
    barrier = pltpu.get_barrier_semaphore()

    def peer(d):
        other = lax.rem(me + d, count)
        return (lax.div(other, ny), lax.rem(other, ny))

    for planes in (x3, g3, a3, h3):
        clear_border(planes)

    def greet(d, carry):
        pl.semaphore_signal(
            barrier, inc=1, device_id=peer(d), device_id_type=pl.DeviceIdType.MESH
        )
        return carry

    lax.fori_loop(1, count, greet, 0)
    _, count_x, count_y, depth, _ = x3.shape
    count_x, count_y = count_x - 2, count_y - 2
    rows = count_y * depth
    slots, width = cot_ref.shape
    channels = w1_ref.shape[1]
    grid = (ix, iy, nx, ny)
    halos = [
        Halo(planes, halo_send.at[k], halo_recv.at[k], grid)
        for k, planes in enumerate((x3, g3, a3, h3))
    ]
    inside = (pl.ds(1, count_x), pl.ds(1, count_y))
    build_move(move, depth)
    pair_weights(w1_ref, tx, True)
    pair_weights(w2_ref, tg, False)
    pair_weights(w2_ref, ta, True)
    pair_weights(w1_ref, th, False)

    hot = (slot_row_ref[...] == iota((slots, in_ref.shape[0]), 0)).astype(F32)
    active = jnp.sum(hot, axis=1, keepdims=True)
    spread_columns(cot_ref[...], active, move, s2, depth)
    g3[1, inside[0], inside[1]] = s2[...].astype(BF16).reshape(count_x, count_y, depth, LANES)
    pl.semaphore_wait(barrier, count - 1)
    halos[1].start()
    got = jnp.dot(hot.astype(BF16), in_ref[:, :width], preferred_element_type=F32).astype(BF16)
    spread_columns(got, None, move, s1, depth)
    x3[1, inside[0], inside[1]] = s1[...].astype(BF16).reshape(count_x, count_y, depth, LANES)
    halos[0].start()
    wide = jnp.broadcast_to(active, (slots, LANES))
    for z in range(depth):
        mask_p[pl.ds(z, slots, stride=depth), :] = wide
    shift_inside(g3)
    shift_inside(x3)
    halos[1].wait()
    shift_border(g3)
    halos[0].wait()
    shift_border(x3)

    def forward(xp, carry):
        hidden2 = pair_conv(x3, tx, xp, count_y)
        grad2 = pair_conv(g3, tg, xp, count_y)
        for p in range(2):
            x = 2 * xp + p
            mask = mask_p[pl.ds(pl.multiple_of(x * rows, rows), rows), :]
            hidden = mask * hidden2[:, p * LANES : (p + 1) * LANES]
            grad = grad2[:, p * LANES : (p + 1) * LANES]
            s = 1.0 / (1.0 + jnp.exp(-hidden))
            a3[1, x + 1, 1 : count_y + 1] = (
                (hidden * s).astype(BF16).reshape(count_y, depth, LANES)
            )
            hg = mask * grad * s * (1.0 + hidden * (1.0 - s))
            h3[1, x + 1, 1 : count_y + 1] = hg.astype(BF16).reshape(count_y, depth, LANES)
        return carry

    lax.fori_loop(0, count_x // 2, forward, 0)
    halos[2].start()
    halos[3].start()
    correlate(h3, x3, turned, grads)
    pack_grads(grads, packed, 0, False, channels)
    correlate(a3, g3, turned, grads)
    pack_grads(grads, packed, 27, True, channels)
    used = 54 * channels * channels // LANES
    packed[used:, :] = jnp.zeros((packed.shape[0] - used, LANES), F32)
    shares[...] = packed[...].astype(BF16).reshape(shares.shape)

    def send_share(d, carry):
        other = lax.rem(me + d, count)
        pltpu.make_async_remote_copy(
            src_ref=shares.at[other],
            dst_ref=spread.at[d - 1],
            send_sem=sum_send.at[0],
            recv_sem=sum_recv.at[0],
            device_id=peer(d),
            device_id_type=pl.DeviceIdType.MESH,
        ).start()
        return carry

    lax.fori_loop(1, count, send_share, 0)
    shift_inside(a3)
    shift_inside(h3)
    halos[2].wait()
    halos[3].wait()
    shift_border(a3)
    shift_border(h3)

    def backward(xp, carry):
        second2 = pair_conv(a3, ta, xp, count_y)
        grad2 = pair_conv(h3, th, xp, count_y)
        for p in range(2):
            x = 2 * xp + p
            at = pl.ds(pl.multiple_of(x * rows, rows), rows)
            own = x3[1, x + 1, 1 : count_y + 1].reshape(rows, LANES).astype(F32)
            cot = g3[1, x + 1, 1 : count_y + 1].reshape(rows, LANES).astype(F32)
            s1[at, :] = own + mask_p[at, :] * second2[:, p * LANES : (p + 1) * LANES]
            s2[at, :] = cot + grad2[:, p * LANES : (p + 1) * LANES]
        return carry

    lax.fori_loop(0, count_x // 2, backward, 0)

    pltpu.make_async_copy(spread, spread, sum_recv.at[0]).wait()
    pltpu.make_async_copy(spread, spread, sum_send.at[0]).wait()
    own_share = shares[me].astype(F32)
    total = lax.fori_loop(
        0, count - 1, lambda d, acc: acc + spread[d].astype(F32), own_share
    )
    whole[me] = total.astype(BF16)

    def send_total(d, carry):
        pltpu.make_async_remote_copy(
            src_ref=whole.at[me],
            dst_ref=whole.at[me],
            send_sem=sum_send.at[1],
            recv_sem=sum_recv.at[1],
            device_id=peer(d),
            device_id_type=pl.DeviceIdType.MESH,
        ).start()
        return carry

    lax.fori_loop(1, count, send_total, 0)

    grad_rows = gather_columns(s2, move, slots, depth)
    back_hot = (slot_col_ref[...] == iota((in_ref.shape[0], slots), 1)).astype(F32).astype(BF16)
    back_ref[...] = jnp.dot(back_hot, grad_rows, preferred_element_type=F32).astype(BF16)
    out_ref[...] = gather_columns(s1, move, slots, depth)

    pltpu.make_async_copy(spread, spread, sum_recv.at[1]).wait()
    pltpu.make_async_copy(spread, spread, sum_send.at[1]).wait()
    packed[...] = whole[...].astype(F32).reshape(packed.shape)
    unpack_grads(packed, dw1_ref, 0, factor, channels)
    unpack_grads(packed, dw2_ref, 27, factor, channels)


def on_device(column_features, column_route, cotangent, first_weight, second_weight):
    count_x = lax.axis_size("rx")
    count_y = lax.axis_size("ry")
    count_all = count_x * count_y
    shard_rows, row_width = column_features.shape
    region_x, region_y = cotangent.shape[:2]
    channels = first_weight.shape[1]
    depth = row_width // channels
    region_slots = region_x * region_y
    capacity = 2 * shard_rows // count_all
    capacity_all = count_all * capacity
    owners = column_route // region_slots
    slot_ids = column_route % region_slots
    shard_index = jnp.arange(shard_rows, dtype=jnp.int32)
    earlier = shard_index[:, None] > shard_index[None, :]
    same_owner = owners[:, None] == owners[None, :]
    ranks = jnp.sum(jnp.logical_and(earlier, same_owner).astype(jnp.int32), axis=1)
    send_pos = owners * capacity + ranks
    buffer_index = jnp.arange(capacity_all, dtype=jnp.int32)
    send_hot = send_pos[:, None] == buffer_index[None, :]
    send_table = send_hot.astype(BF16)
    outgoing = jnp.einsum(
        "sr,sw->rw", send_table, column_features, preferred_element_type=F32
    ).astype(BF16)
    filled = jnp.sum(send_hot.astype(jnp.int32), axis=0)
    slot_total = jnp.sum(jnp.where(send_hot, slot_ids[:, None], 0), axis=0)
    out_slots = jnp.where(filled > 0, slot_total, region_slots).astype(BF16)
    outgoing = jnp.concatenate(
        [outgoing, jnp.broadcast_to(out_slots[:, None], (capacity_all, LANES))], axis=1
    )
    incoming = lax.all_to_all(
        outgoing.reshape(count_all, capacity, row_width + LANES),
        ("rx", "ry"),
        split_axis=0,
        concat_axis=0,
        tiled=True,
    ).reshape(capacity_all, row_width + LANES)
    in_slots = incoming[:, row_width].astype(jnp.int32)

    cot_rows = cotangent.reshape(region_slots, row_width)
    planes = pltpu.VMEM((3, region_x + 2, region_y + 2, depth, LANES), BF16)
    table = pltpu.VMEM((36 * LANES, 2 * LANES), BF16)
    voxels = region_slots * depth
    padded = -(-(54 * channels * channels // LANES) // (16 * count_all)) * 16 * count_all
    share = padded // count_all
    factor = float(1.0 / (count_all * shard_rows * depth) ** 0.5)
    row_shape = jax.ShapeDtypeStruct((region_slots, row_width), BF16)
    grad_shape = jax.ShapeDtypeStruct((27, channels, channels), F32)
    out_rows, back_rows, first_grad, second_grad = pl.pallas_call(
        functools.partial(core_kernel, count_x, count_y, factor),
        out_shape=(
            row_shape,
            jax.ShapeDtypeStruct((capacity_all, row_width), BF16),
            grad_shape,
            grad_shape,
        ),
        in_specs=[pl.BlockSpec(memory_space=pltpu.VMEM)] * 6,
        out_specs=[pl.BlockSpec(memory_space=pltpu.VMEM)] * 4,
        scratch_shapes=[
            planes, planes, planes, planes,
            table, table, table, table,
            pltpu.VMEM((row_width, depth * LANES), BF16),
            pltpu.VMEM((voxels, LANES), F32),
            pltpu.VMEM((voxels, LANES), F32),
            pltpu.VMEM((voxels, LANES), F32),
            pltpu.VMEM((2 * LANES, voxels // 2), BF16),
            pltpu.VMEM((45, LANES, LANES), F32),
            pltpu.VMEM((padded, LANES), F32),
            pltpu.VMEM((count_all, share, LANES), BF16),
            pltpu.VMEM((count_all - 1, share, LANES), BF16),
            pltpu.VMEM((count_all, share, LANES), BF16),
            pltpu.SemaphoreType.DMA((4, len(SIDES))),
            pltpu.SemaphoreType.DMA((4, len(SIDES))),
            pltpu.SemaphoreType.DMA((2,)),
            pltpu.SemaphoreType.DMA((2,)),
        ],
        compiler_params=pltpu.CompilerParams(
            vmem_limit_bytes=VMEM_LIMIT, collective_id=1, has_side_effects=True
        ),
    )(
        incoming, in_slots[None, :], in_slots[:, None], cot_rows, first_weight, second_weight
    )
    returned = lax.all_to_all(
        back_rows.reshape(count_all, capacity, row_width),
        ("rx", "ry"),
        split_axis=0,
        concat_axis=0,
        tiled=True,
    ).reshape(capacity_all, row_width)
    feature_grads = jnp.dot(send_table, returned, preferred_element_type=F32).astype(BF16)
    return (
        out_rows.reshape(region_x, region_y, row_width),
        feature_grads,
        first_grad,
        second_grad,
    )


def solution(mesh):
    in_specs = (P(("rx", "ry"), None), P(("rx", "ry")), P("rx", "ry", None), P(), P())
    out_specs = (P("rx", "ry", None), P(("rx", "ry"), None), P(), P())
    return jax.shard_map(
        on_device, mesh=mesh, in_specs=in_specs, out_specs=out_specs, check_vma=False
    )
```

time: 386 us -> 151 us (0.39); the launches traced: 379 us -> 150 us
  waiting for transfers between devices: 152 us -> 16.4 us
  starting transfers between devices: 68.5 us -> 7.04 us
  local copies, waits for them, and re-layouts: 32.6 us -> 7.75 us
  Pallas kernels: 63 us -> 84.9 us
  other arithmetic: 18.2 us -> 2.49 us
  between operations: 14.8 us -> 0.76 us
    unnamed x2 -> x0, waiting for transfers between devices: 135 us -> none
    ppermute x16 -> x0, starting transfers between devices: 40.8 us -> none  [the longest x8 27.7 us: extended(): lax.ppermute(lax.slice_in_dim(block, block.shape[dim] - width, None, axis...]
    pallas_call x3 -> x1, Pallas kernels: 63 us -> 84.9 us  [on_device(): pl.pallas_call(functools.partial(core_kernel, count_x, count_y, factor),...]
    all_to_all x1 -> x0, starting transfers between devices: 12 us -> none  [on_device(): lax.all_to_all(both, ('rx', 'ry'), split_axis=0, concat_axis=0, tiled=True)]
    all_to_all x1, starting transfers between devices: 15.7 us -> 7.04 us  [on_device(): lax.all_to_all(back_rows.reshape(count_all, capacity, row_width), ('rx',...]
    slice x12 -> x0, local copies, waits for them, and re-layouts: 7.09 us -> none  [the longest x4 2.66 us: extended(): lax.slice_in_dim(block, 0, width, axis=dim)]
    convert_element_type x1 -> x0, other arithmetic: 7.08 us -> none  [on_device(): jnp.stack([first_local, second_local]).astype(BF16).reshape(count_all, -1)]
    convert_element_type x2 -> x0, local copies, waits for them, and re-layouts: 6.41 us -> none  [on_device(): jnp.stack([first_local, second_local]).astype(BF16).reshape(count_all, -1)]
  transfers between devices with their start and end apart: 19 -> 1, of which waited for: 5 -> 1; matrix products, arithmetic and copies ran while one was open for 5% -> 0% of each run, Pallas kernels for 6% -> 0%
where the time goes in v2:
time: 151 us; the launch traced here: 150 us
  Pallas kernels  84.9 us (56%)
  blocking collectives  28.4 us (19%)
  waiting for transfers between devices  16.4 us (11%)
  local copies, waits for them, and re-layouts  7.75 us (5%)
  starting transfers between devices  7.04 us (5%)
  matrix products  2.52 us (2%)
  other arithmetic  2.49 us (2%)
    pallas_call x1, Pallas kernels, on_device(): pl.pallas_call(functools.partial(core_kernel, count_x, count_y, factor),...  84.9 us
    all_to_all x1, blocking collectives, on_device(): lax.all_to_all(outgoing.reshape(count_all, capacity, row_width + LANES),...  28.4 us
    all_to_all x1, waiting for transfers between devices, on_device(): lax.all_to_all(back_rows.reshape(count_all, capacity, row_width), ('rx',...  16.4 us
    all_to_all x1, starting transfers between devices, on_device(): lax.all_to_all(back_rows.reshape(count_all, capacity, row_width), ('rx',...  7.04 us
    unnamed x15, local copies, waits for them, and re-layouts  3.86 us
  transfers between devices with their start and end apart: 1, of which 1 were waited for; matrix products, arithmetic and copies ran while one was open for 0% of the time, Pallas kernels for 0%

profile of v2, /device:TPU:1, one launch (start us, length us, event | category | flops | bytes accessed | tf_op | source)
XLA Modules:
  0.0 150.3 jit_solution(8119906543559464334)
XLA Ops:
  0.6 0.7 and_select_fusion
  1.3 0.2 convert_reduce_fusion.1
  1.5 0.0 copy-start.4
  1.5 0.1 convert_reduce_fusion
  1.6 1.5 convolution_convert_fusion
  3.1 0.0 copy-done.4
  3.1 0.1 broadcast_in_dim.21
  3.2 0.1 pad_maximum_fusion
  3.3 0.3 reshape.49
  3.6 28.4 %all_to_all.10 = bf16[128,2,1664]{2,1,0:T(2,128)(2,1)S(1)} all-to-all(bf16[128,2,1664]{2,1,0:T(2,128)(2,1)S(1)} %reshape.49), channel_id=1, replica_groups=mesh['rx'=8,'ry'=16] {'rx','ry'}, dimensions={0} | all-to-all | bytes 1703936 | tf_op jit(solution)/shard_map/all_to_all | solution.py:437
  32.0 0.3 reshape.50.in_ref
  32.3 0.0 copy-start
  32.3 0.8 fusion.3
  33.1 0.1 copy-done
  33.2 0.7 slice_convert_fusion.slot_col_ref
  33.9 84.9 %shard_map.84 = (bf16[256,1536]{1,0:T(8,128)(2,1)}, bf16[256,1536]{1,0:T(8,128)(2,1)}, f32[27,96,96]{2,1,0:T(8,128)}, f32[27,96,96]{2,1,0:T(8,128)}) custom-call(bf16[256,1664]{1,0:T(8,128)(2,1)} %copy-done, s32[1,256]{1,0:T(1,128)} %bitcast.7, s32[256,1]{1,0:T(8,128)} %slice_convert_fusion.slot_col_ref, bf16[256,1536]{1,0:T(8,128)(2,1)} %bitcast.6, ...), custom_call_target="tpu_custom_call" | custom-call | tf_op jit(solution)/shard_map/pallas_call | solution.py:455
  118.8 2.9 %reshape.53 = bf16[128,2,1536]{2,1,0:T(2,128)(2,1)} reshape(bf16[256,1536]{1,0:T(8,128)(2,1)} %get-tuple-element.9) | data formatting | bytes 1572864 | tf_op jit(solution)/shard_map/reshape | solution.py:490
  121.6 0.0 copy-start.5
  121.6 7.0 %all-to-all-start.1 = ((bf16[128,2,1536]{2,1,0:T(2,128)(2,1)}), bf16[128,2,1536]{2,1,0:T(2,128)(2,1)S(1)}, u32[]{:S(2)}, u32[]{:S(2)}) async-start(bf16[128,2,1536]{2,1,0:T(2,128)(2,1)} %reshape.53), calls=%async_computation.1 | async-start | bytes 1572864 | tf_op jit(solution)/shard_map/all_to_all | solution.py:489
  128.7 0.0 copy-start.3
  128.7 16.4 %all-to-all-done.1 = bf16[128,2,1536]{2,1,0:T(2,128)(2,1)S(1)} async-done(((bf16[128,2,1536]{2,1,0:T(2,128)(2,1)}), bf16[128,2,1536]{2,1,0:T(2,128)(2,1)S(1)}, u32[]{:S(2)}, u32[]{:S(2)}) %all-to-all-start.1) | async-done | bytes 786464 | tf_op jit(solution)/shard_map/all_to_all | solution.py:489
  145.1 0.3 reshape.54
  145.4 0.0 copy-done.5
  145.4 0.0 copy-start.2
  145.5 1.1 convolution_convert_fusion.1
  146.5 0.0 copy-done.3
  146.5 0.9 copy.12
  147.4 0.0 copy-done.2
  147.4 0.0 copy-start.1
  147.4 1.1 copy.13
  148.5 0.7 copy-done.1
  149.2 1.1 copy.14
  (2 shorter events, 0.0 us)
Async XLA Ops:
  1.5 1.6 %copy-start.4 = (s32[128]{0:T(128)}, s32[128]{0:T(128)S(1)}, u32[]{:S(2)}) copy-start(s32[128]{0:T(128)S(1)} %multiply_add_fusion) | copy-start | bytes 1540
  32.3 0.9 copy-start
  121.6 23.8 %copy-start.5 = (s32[128]{0:T(128)S(1)}, s32[128]{0:T(128)}, u32[]{:S(2)}) copy-start(s32[128]{0:T(128)} %copy-done.4) | copy-start | bytes 1540
  121.6 23.5 %all-to-all-start.1 = ((bf16[128,2,1536]{2,1,0:T(2,128)(2,1)}), bf16[128,2,1536]{2,1,0:T(2,128)(2,1)S(1)}, u32[]{:S(2)}, u32[]{:S(2)}) async-start(bf16[128,2,1536]{2,1,0:T(2,128)(2,1)} %reshape.53), calls=%async_computation.1 | async-start | bytes 1572864 | tf_op jit(solution)/shard_map/all_to_all | solution.py:489
  128.7 17.8 %copy-start.3 = (bf16[256,1536]{1,0:T(8,128)(2,1)S(1)}, bf16[256,1536]{1,0:T(8,128)(2,1)}, u32[]{:S(2)}) copy-start(bf16[256,1536]{1,0:T(8,128)(2,1)} %get-tuple-element.8) | copy-start | bytes 2359300
  145.4 2.0 %copy-start.2 = (f32[27,96,96]{2,1,0:T(8,128)S(1)}, f32[27,96,96]{2,1,0:T(8,128)}, u32[]{:S(2)}) copy-start(f32[27,96,96]{2,1,0:T(8,128)} %get-tuple-element.22) | copy-start | bytes 2985988
  147.4 1.8 %copy-start.1 = (f32[27,96,96]{2,1,0:T(8,128)S(1)}, f32[27,96,96]{2,1,0:T(8,128)}, u32[]{:S(2)}) copy-start(f32[27,96,96]{2,1,0:T(8,128)} %get-tuple-element.23) | copy-start | bytes 2985988

commit v3 on v2

--- a/solution.py
+++ b/solution.py
@@ -246,18 +246,52 @@
                 self.copy(k).wait_send()
 
 
+def lay_messages(parts, scratch, dest):
+    devices, height, _ = dest.shape
+    pitch = scratch.shape[0] // devices
+    for row, value in enumerate(parts):
+        scratch[pl.ds(row, devices, stride=pitch), :] = value
+    flat = scratch[...].reshape(devices, pitch, LANES)
+    dest[...] = flat[:, :height].astype(BF16)
+
+
+def read_messages(source, scratch, capacity):
+    devices, height, _ = source.shape
+    pitch = scratch.shape[0] // devices
+    each = height // capacity
+    filler = jnp.zeros((devices, pitch - height, LANES), F32)
+    scratch[...] = jnp.concatenate([source[...].astype(F32), filler], axis=1).reshape(
+        scratch.shape
+    )
+    return jnp.concatenate(
+        [
+            jnp.concatenate(
+                [
+                    scratch[pl.ds(k * each + j, devices, stride=pitch), :].astype(BF16)
+                    for j in range(each)
+                ],
+                axis=1,
+            )
+            for k in range(capacity)
+        ],
+        axis=0,
+    )
+
+
 def core_kernel(
-    nx, ny, factor,
-    in_ref, slot_row_ref, slot_col_ref, cot_ref, w1_ref, w2_ref,
-    out_ref, back_ref, dw1_ref, dw2_ref,
+    nx, ny, capacity, factor,
+    feat_ref, route_row_ref, route_col_ref, cot_ref, w1_ref, w2_ref,
+    out_ref, fg_ref, dw1_ref, dw2_ref,
     x3, g3, a3, h3, tx, tg, ta, th, move, s1, s2, mask_p, turned, grads,
     packed, shares, spread, whole,
-    halo_send, halo_recv, sum_send, sum_recv,
+    sent, got, back_sent, back_got, routes,
+    halo_send, halo_recv, sum_send, sum_recv, col_send, col_recv,
 ):
     ix, iy = lax.axis_index("rx"), lax.axis_index("ry")
     count = nx * ny
     me = ix * ny + iy
     barrier = pltpu.get_barrier_semaphore()
+    mesh_id = pl.DeviceIdType.MESH
 
     def peer(d):
         other = lax.rem(me + d, count)
@@ -267,9 +301,7 @@
         clear_border(planes)
 
     def greet(d, carry):
-        pl.semaphore_signal(
-            barrier, inc=1, device_id=peer(d), device_id_type=pl.DeviceIdType.MESH
-        )
+        pl.semaphore_signal(barrier, inc=1, device_id=peer(d), device_id_type=mesh_id)
         return carry
 
     lax.fori_loop(1, count, greet, 0)
@@ -277,6 +309,7 @@
     count_x, count_y = count_x - 2, count_y - 2
     rows = count_y * depth
     slots, width = cot_ref.shape
+    shard = feat_ref.shape[0]
     channels = w1_ref.shape[1]
     grid = (ix, iy, nx, ny)
     halos = [
@@ -284,124 +317,253 @@
         for k, planes in enumerate((x3, g3, a3, h3))
     ]
     inside = (pl.ds(1, count_x), pl.ds(1, count_y))
+
+    row, col = route_row_ref[...], route_col_ref[...]
+    owner_row, owner_col = lax.div(row, slots), lax.div(col, slots)
+    same = owner_col == owner_row
+    s0, s1_ = iota((shard, shard), 0), iota((shard, shard), 1)
+    rank_row = jnp.sum(jnp.where(same & (s0 < s1_), 1.0, 0.0), axis=0, keepdims=True)
+    rank_col = jnp.sum(jnp.where(same & (s1_ < s0), 1.0, 0.0), axis=1, keepdims=True)
+    ahead_row = lax.rem(owner_row - me + count, count)
+    ahead_col = lax.rem(owner_col - me + count, count)
+    place_row = rank_row.astype(jnp.int32) * count + ahead_row
+    place_col = rank_col.astype(jnp.int32) * count + ahead_col
+    buffer = capacity * count
+    send_hot = jnp.where(iota((buffer, shard), 0) == place_row, 1.0, 0.0).astype(BF16)
+    return_hot = jnp.where(iota((shard, buffer), 1) == place_col, 1.0, 0.0).astype(BF16)
+    outgoing = jnp.dot(send_hot, feat_ref[...], preferred_element_type=F32)
+    lay_messages(
+        [
+            outgoing[k * count : (k + 1) * count, j * LANES : (j + 1) * LANES]
+            for k in range(capacity)
+            for j in range(width // LANES)
+        ],
+        s1,
+        sent,
+    )
+    routes[0] = row
+    got[0] = sent[0]
+    pl.semaphore_wait(barrier, count - 1)
+
+    def send_route(d, carry):
+        pltpu.make_async_remote_copy(
+            src_ref=route_row_ref,
+            dst_ref=routes.at[d],
+            send_sem=col_send.at[0],
+            recv_sem=col_recv.at[0],
+            device_id=peer(d),
+            device_id_type=mesh_id,
+        ).start()
+        return carry
+
+    def send_column(d, carry):
+        pltpu.make_async_remote_copy(
+            src_ref=sent.at[d],
+            dst_ref=got.at[d],
+            send_sem=col_send.at[1],
+            recv_sem=col_recv.at[1],
+            device_id=peer(d),
+            device_id_type=mesh_id,
+        ).start()
+        return carry
+
+    def wait_all(ref, sem):
+        pltpu.make_async_copy(ref.at[pl.ds(1, count - 1)], ref.at[pl.ds(1, count - 1)], sem).wait()
+
+    lax.fori_loop(1, count, send_route, 0)
+    lax.fori_loop(1, count, send_column, 0)
+
     build_move(move, depth)
-    pair_weights(w1_ref, tx, True)
+    spread_columns(cot_ref[...], None, move, s2, depth)
     pair_weights(w2_ref, tg, False)
-    pair_weights(w2_ref, ta, True)
-    pair_weights(w1_ref, th, False)
-
-    hot = (slot_row_ref[...] == iota((slots, in_ref.shape[0]), 0)).astype(F32)
+    wait_all(routes, col_recv.at[0])
+
+    known = routes[...].reshape(count, shard)
+    mine = lax.div(known, slots) == me
+    mine_f = jnp.where(mine, 1.0, 0.0)
+    upper = jnp.where(s0 < s1_, 1.0, 0.0).astype(BF16)
+    before = jnp.dot(mine_f.astype(BF16), upper, preferred_element_type=F32)
+    slot_of = lax.rem(known, slots).astype(F32)
+    slot_cols, slot_rows = [], []
+    for k in range(capacity):
+        chosen = mine & (before == float(k))
+        found = jnp.sum(jnp.where(chosen, slot_of + 1.0, 0.0), axis=1, keepdims=True) - 1.0
+        slot_cols.append(found)
+        slot_rows.append(jnp.broadcast_to(found, (count, LANES)).T[:1, :])
+    slot_row = jnp.concatenate(slot_rows, axis=1).astype(jnp.int32)
+    slot_col = jnp.concatenate(slot_cols, axis=0).astype(jnp.int32)
+    hot = jnp.where(slot_row == iota((slots, buffer), 0), 1.0, 0.0)
+    back_hot = jnp.where(slot_col == iota((buffer, slots), 1), 1.0, 0.0).astype(BF16)
     active = jnp.sum(hot, axis=1, keepdims=True)
-    spread_columns(cot_ref[...], active, move, s2, depth)
-    g3[1, inside[0], inside[1]] = s2[...].astype(BF16).reshape(count_x, count_y, depth, LANES)
-    pl.semaphore_wait(barrier, count - 1)
-    halos[1].start()
-    got = jnp.dot(hot.astype(BF16), in_ref[:, :width], preferred_element_type=F32).astype(BF16)
-    spread_columns(got, None, move, s1, depth)
-    x3[1, inside[0], inside[1]] = s1[...].astype(BF16).reshape(count_x, count_y, depth, LANES)
-    halos[0].start()
     wide = jnp.broadcast_to(active, (slots, LANES))
     for z in range(depth):
         mask_p[pl.ds(z, slots, stride=depth), :] = wide
+    g3[1, inside[0], inside[1]] = (
+        (s2[...] * mask_p[...]).astype(BF16).reshape(count_x, count_y, depth, LANES)
+    )
+    halos[1].start()
     shift_inside(g3)
-    shift_inside(x3)
+    pair_weights(w1_ref, tx, True)
+    pair_weights(w2_ref, ta, True)
+    pair_weights(w1_ref, th, False)
     halos[1].wait()
     shift_border(g3)
+
+    wait_all(got, col_recv.at[1])
+    arrived = read_messages(got, s1, capacity)
+    field_rows = jnp.dot(hot.astype(BF16), arrived, preferred_element_type=F32).astype(BF16)
+    spread_columns(field_rows, None, move, s1, depth)
+    x3[1, inside[0], inside[1]] = s1[...].astype(BF16).reshape(count_x, count_y, depth, LANES)
+    halos[0].start()
+    shift_inside(x3)
+
+    def conv_to(planes, table, dest):
+        def body(xp, carry):
+            both = pair_conv(planes, table, xp, count_y)
+            for p in range(2):
+                at = pl.ds(pl.multiple_of((2 * xp + p) * rows, rows), rows)
+                dest[at, :] = both[:, p * LANES : (p + 1) * LANES]
+            return carry
+
+        lax.fori_loop(0, count_x // 2, body, 0)
+
+    conv_to(g3, tg, s2)
     halos[0].wait()
     shift_border(x3)
 
     def forward(xp, carry):
         hidden2 = pair_conv(x3, tx, xp, count_y)
-        grad2 = pair_conv(g3, tg, xp, count_y)
         for p in range(2):
             x = 2 * xp + p
-            mask = mask_p[pl.ds(pl.multiple_of(x * rows, rows), rows), :]
+            at = pl.ds(pl.multiple_of(x * rows, rows), rows)
+            mask = mask_p[at, :]
             hidden = mask * hidden2[:, p * LANES : (p + 1) * LANES]
-            grad = grad2[:, p * LANES : (p + 1) * LANES]
             s = 1.0 / (1.0 + jnp.exp(-hidden))
             a3[1, x + 1, 1 : count_y + 1] = (
                 (hidden * s).astype(BF16).reshape(count_y, depth, LANES)
             )
-            hg = mask * grad * s * (1.0 + hidden * (1.0 - s))
+            hg = mask * s2[at, :] * s * (1.0 + hidden * (1.0 - s))
             h3[1, x + 1, 1 : count_y + 1] = hg.astype(BF16).reshape(count_y, depth, LANES)
         return carry
 
     lax.fori_loop(0, count_x // 2, forward, 0)
+    halos[3].start()
     halos[2].start()
-    halos[3].start()
-    correlate(h3, x3, turned, grads)
-    pack_grads(grads, packed, 0, False, channels)
-    correlate(a3, g3, turned, grads)
-    pack_grads(grads, packed, 27, True, channels)
-    used = 54 * channels * channels // LANES
+    used = 27 * channels * channels // LANES
     packed[used:, :] = jnp.zeros((packed.shape[0] - used, LANES), F32)
-    shares[...] = packed[...].astype(BF16).reshape(shares.shape)
-
-    def send_share(d, carry):
-        other = lax.rem(me + d, count)
+
+    def sum_out(half, local, planes, flip):
+        correlate(local, planes, turned, grads)
+        pack_grads(grads, packed, 0, flip, channels)
+        shares[half] = packed[...].astype(BF16).reshape(shares.shape[1:])
+
+        def send_share(d, carry):
+            other = lax.rem(me + d, count)
+            pltpu.make_async_remote_copy(
+                src_ref=shares.at[half, other],
+                dst_ref=spread.at[half, d],
+                send_sem=sum_send.at[half],
+                recv_sem=sum_recv.at[half],
+                device_id=peer(d),
+                device_id_type=mesh_id,
+            ).start()
+            return carry
+
+        lax.fori_loop(1, count, send_share, 0)
+
+    sum_out(0, h3, x3, False)
+    sum_out(1, a3, g3, True)
+    shift_inside(h3)
+    shift_inside(a3)
+    halos[3].wait()
+    shift_border(h3)
+
+    def grad_body(xp, carry):
+        both = pair_conv(h3, th, xp, count_y)
+        for p in range(2):
+            x = 2 * xp + p
+            at = pl.ds(pl.multiple_of(x * rows, rows), rows)
+            cot = g3[1, x + 1, 1 : count_y + 1].reshape(rows, LANES).astype(F32)
+            s2[at, :] = cot + both[:, p * LANES : (p + 1) * LANES]
+        return carry
+
+    lax.fori_loop(0, count_x // 2, grad_body, 0)
+    grad_rows = gather_columns(s2, move, slots, depth)
+    back_rows = jnp.dot(back_hot, grad_rows, preferred_element_type=F32)
+    lay_messages(
+        [
+            back_rows[k * count : (k + 1) * count, j * LANES : (j + 1) * LANES]
+            for k in range(capacity)
+            for j in range(width // LANES)
+        ],
+        s1,
+        back_sent,
+    )
+    back_got[0] = back_sent[0]
+
+    def send_back(d, carry):
         pltpu.make_async_remote_copy(
-            src_ref=shares.at[other],
-            dst_ref=spread.at[d - 1],
-            send_sem=sum_send.at[0],
-            recv_sem=sum_recv.at[0],
-            device_id=peer(d),
-            device_id_type=pl.DeviceIdType.MESH,
+            src_ref=back_sent.at[d],
+            dst_ref=back_got.at[d],
+            send_sem=col_send.at[2],
+            recv_sem=col_recv.at[2],
+            device_id=peer(count - d),
+            device_id_type=mesh_id,
         ).start()
         return carry
 
-    lax.fori_loop(1, count, send_share, 0)
-    shift_inside(a3)
-    shift_inside(h3)
+    lax.fori_loop(1, count, send_back, 0)
+
+    for half in range(2):
+        wait_all(spread.at[half], sum_recv.at[half])
+        own_share = shares[half, me].astype(F32)
+        total = lax.fori_loop(
+            1, count, lambda d, acc: acc + spread[half, d].astype(F32), own_share
+        )
+        whole[half, me] = total.astype(BF16)
+
+        def send_total(d, carry):
+            pltpu.make_async_remote_copy(
+                src_ref=whole.at[half, me],
+                dst_ref=whole.at[half, me],
+                send_sem=sum_send.at[2 + half],
+                recv_sem=sum_recv.at[2 + half],
+                device_id=peer(d),
+                device_id_type=mesh_id,
+            ).start()
+            return carry
+
+        lax.fori_loop(1, count, send_total, 0)
+
     halos[2].wait()
-    halos[3].wait()
     shift_border(a3)
-    shift_border(h3)
-
-    def backward(xp, carry):
-        second2 = pair_conv(a3, ta, xp, count_y)
-        grad2 = pair_conv(h3, th, xp, count_y)
+
+    def block_body(xp, carry):
+        both = pair_conv(a3, ta, xp, count_y)
         for p in range(2):
             x = 2 * xp + p
             at = pl.ds(pl.multiple_of(x * rows, rows), rows)
             own = x3[1, x + 1, 1 : count_y + 1].reshape(rows, LANES).astype(F32)
-            cot = g3[1, x + 1, 1 : count_y + 1].reshape(rows, LANES).astype(F32)
-            s1[at, :] = own + mask_p[at, :] * second2[:, p * LANES : (p + 1) * LANES]
-            s2[at, :] = cot + grad2[:, p * LANES : (p + 1) * LANES]
-        return carry
-
-    lax.fori_loop(0, count_x // 2, backward, 0)
-
-    pltpu.make_async_copy(spread, spread, sum_recv.at[0]).wait()
-    pltpu.make_async_copy(spread, spread, sum_send.at[0]).wait()
-    own_share = shares[me].astype(F32)
-    total = lax.fori_loop(
-        0, count - 1, lambda d, acc: acc + spread[d].astype(F32), own_share
-    )
-    whole[me] = total.astype(BF16)
-
-    def send_total(d, carry):
-        pltpu.make_async_remote_copy(
-            src_ref=whole.at[me],
-            dst_ref=whole.at[me],
-            send_sem=sum_send.at[1],
-            recv_sem=sum_recv.at[1],
-            device_id=peer(d),
-            device_id_type=pl.DeviceIdType.MESH,
-        ).start()
-        return carry
-
-    lax.fori_loop(1, count, send_total, 0)
-
-    grad_rows = gather_columns(s2, move, slots, depth)
-    back_hot = (slot_col_ref[...] == iota((in_ref.shape[0], slots), 1)).astype(F32).astype(BF16)
-    back_ref[...] = jnp.dot(back_hot, grad_rows, preferred_element_type=F32).astype(BF16)
+            s1[at, :] = own + mask_p[at, :] * both[:, p * LANES : (p + 1) * LANES]
+        return carry
+
+    lax.fori_loop(0, count_x // 2, block_body, 0)
     out_ref[...] = gather_columns(s1, move, slots, depth)
 
-    pltpu.make_async_copy(spread, spread, sum_recv.at[1]).wait()
-    pltpu.make_async_copy(spread, spread, sum_send.at[1]).wait()
-    packed[...] = whole[...].astype(F32).reshape(packed.shape)
-    unpack_grads(packed, dw1_ref, 0, factor, channels)
-    unpack_grads(packed, dw2_ref, 27, factor, channels)
+    wait_all(back_got, col_recv.at[2])
+    returned = read_messages(back_got, s2, capacity)
+    fg_ref[...] = jnp.dot(return_hot, returned, preferred_element_type=F32).astype(BF16)
+
+    for half, dest in enumerate((dw1_ref, dw2_ref)):
+        wait_all(whole.at[half], sum_recv.at[2 + half])
+        packed[...] = whole[half].astype(F32).reshape(packed.shape)
+        unpack_grads(packed, dest, 0, factor, channels)
+    wait_all(routes, col_send.at[0])
+    wait_all(got, col_send.at[1])
+    wait_all(back_got, col_send.at[2])
+    for half in range(2):
+        wait_all(spread.at[half], sum_send.at[half])
+        wait_all(whole.at[half], sum_send.at[2 + half])
 
 
 def on_device(column_features, column_route, cotangent, first_weight, second_weight):
@@ -414,49 +576,20 @@
     depth = row_width // channels
     region_slots = region_x * region_y
     capacity = 2 * shard_rows // count_all
-    capacity_all = count_all * capacity
-    owners = column_route // region_slots
-    slot_ids = column_route % region_slots
-    shard_index = jnp.arange(shard_rows, dtype=jnp.int32)
-    earlier = shard_index[:, None] > shard_index[None, :]
-    same_owner = owners[:, None] == owners[None, :]
-    ranks = jnp.sum(jnp.logical_and(earlier, same_owner).astype(jnp.int32), axis=1)
-    send_pos = owners * capacity + ranks
-    buffer_index = jnp.arange(capacity_all, dtype=jnp.int32)
-    send_hot = send_pos[:, None] == buffer_index[None, :]
-    send_table = send_hot.astype(BF16)
-    outgoing = jnp.einsum(
-        "sr,sw->rw", send_table, column_features, preferred_element_type=F32
-    ).astype(BF16)
-    filled = jnp.sum(send_hot.astype(jnp.int32), axis=0)
-    slot_total = jnp.sum(jnp.where(send_hot, slot_ids[:, None], 0), axis=0)
-    out_slots = jnp.where(filled > 0, slot_total, region_slots).astype(BF16)
-    outgoing = jnp.concatenate(
-        [outgoing, jnp.broadcast_to(out_slots[:, None], (capacity_all, LANES))], axis=1
-    )
-    incoming = lax.all_to_all(
-        outgoing.reshape(count_all, capacity, row_width + LANES),
-        ("rx", "ry"),
-        split_axis=0,
-        concat_axis=0,
-        tiled=True,
-    ).reshape(capacity_all, row_width + LANES)
-    in_slots = incoming[:, row_width].astype(jnp.int32)
-
-    cot_rows = cotangent.reshape(region_slots, row_width)
     planes = pltpu.VMEM((3, region_x + 2, region_y + 2, depth, LANES), BF16)
     table = pltpu.VMEM((36 * LANES, 2 * LANES), BF16)
     voxels = region_slots * depth
-    padded = -(-(54 * channels * channels // LANES) // (16 * count_all)) * 16 * count_all
-    share = padded // count_all
+    flat = pltpu.VMEM((voxels, LANES), F32)
+    padded = -(-(27 * channels * channels // LANES) // (16 * count_all)) * 16 * count_all
+    share = pltpu.VMEM((2, count_all, padded // count_all, LANES), BF16)
+    messages = pltpu.VMEM((count_all, capacity * row_width // LANES, LANES), BF16)
     factor = float(1.0 / (count_all * shard_rows * depth) ** 0.5)
-    row_shape = jax.ShapeDtypeStruct((region_slots, row_width), BF16)
     grad_shape = jax.ShapeDtypeStruct((27, channels, channels), F32)
-    out_rows, back_rows, first_grad, second_grad = pl.pallas_call(
-        functools.partial(core_kernel, count_x, count_y, factor),
+    out_rows, feature_grads, first_grad, second_grad = pl.pallas_call(
+        functools.partial(core_kernel, count_x, count_y, capacity, factor),
         out_shape=(
-            row_shape,
-            jax.ShapeDtypeStruct((capacity_all, row_width), BF16),
+            jax.ShapeDtypeStruct((region_slots, row_width), BF16),
+            jax.ShapeDtypeStruct((shard_rows, row_width), BF16),
             grad_shape,
             grad_shape,
         ),
@@ -466,34 +599,31 @@
             planes, planes, planes, planes,
             table, table, table, table,
             pltpu.VMEM((row_width, depth * LANES), BF16),
-            pltpu.VMEM((voxels, LANES), F32),
-            pltpu.VMEM((voxels, LANES), F32),
-            pltpu.VMEM((voxels, LANES), F32),
+            flat, flat, flat,
             pltpu.VMEM((2 * LANES, voxels // 2), BF16),
             pltpu.VMEM((45, LANES, LANES), F32),
             pltpu.VMEM((padded, LANES), F32),
-            pltpu.VMEM((count_all, share, LANES), BF16),
-            pltpu.VMEM((count_all - 1, share, LANES), BF16),
-            pltpu.VMEM((count_all, share, LANES), BF16),
+            share, share, share,
+            messages, messages, messages, messages,
+            pltpu.VMEM((count_all, 1, shard_rows), jnp.int32),
             pltpu.SemaphoreType.DMA((4, len(SIDES))),
             pltpu.SemaphoreType.DMA((4, len(SIDES))),
-            pltpu.SemaphoreType.DMA((2,)),
-            pltpu.SemaphoreType.DMA((2,)),
+            pltpu.SemaphoreType.DMA((4,)),
+            pltpu.SemaphoreType.DMA((4,)),
+            pltpu.SemaphoreType.DMA((3,)),
+            pltpu.SemaphoreType.DMA((3,)),
         ],
         compiler_params=pltpu.CompilerParams(
             vmem_limit_bytes=VMEM_LIMIT, collective_id=1, has_side_effects=True
         ),
     )(
-        incoming, in_slots[None, :], in_slots[:, None], cot_rows, first_weight, second_weight
-    )
-    returned = lax.all_to_all(
-        back_rows.reshape(count_all, capacity, row_width),
-        ("rx", "ry"),
-        split_axis=0,
-        concat_axis=0,
-        tiled=True,
-    ).reshape(capacity_all, row_width)
-    feature_grads = jnp.dot(send_table, returned, preferred_element_type=F32).astype(BF16)
+        column_features,
+        column_route[None, :],
+        column_route[:, None],
+        cotangent.reshape(region_slots, row_width),
+        first_weight,
+        second_weight,
+    )
     return (
         out_rows.reshape(region_x, region_y, row_width),
         feature_grads,

time: 151 us -> 120 us (0.79)
  blocking collectives: 28.4 us -> 0 us
  Pallas kernels: 84.9 us -> 111 us
  waiting for transfers between devices: 16.4 us -> 0 us
  starting transfers between devices: 7.04 us -> 0 us
  matrix products: 2.52 us -> 0 us
  other arithmetic: 2.49 us -> 0 us
    all_to_all x1 -> x0, blocking collectives: 28.4 us -> none  [on_device(): lax.all_to_all(outgoing.reshape(count_all, capacity, row_width + LANES),...]
    pallas_call x1, Pallas kernels: 84.9 us -> 111 us  [on_device(): pl.pallas_call(functools.partial(core_kernel, count_x, count_y, capacity,...]
    all_to_all x1 -> x0, waiting for transfers between devices: 16.4 us -> none  [on_device(): lax.all_to_all(back_rows.reshape(count_all, capacity, row_width), ('rx',...]
    all_to_all x1 -> x0, starting transfers between devices: 7.04 us -> none  [on_device(): lax.all_to_all(back_rows.reshape(count_all, capacity, row_width), ('rx',...]
    reshape x4 -> x0, local copies, waits for them, and re-layouts: 3.79 us -> none  [the longest x1 2.85 us: on_device(): back_rows.reshape(count_all, capacity, row_width)]
    unnamed x15 -> x8, local copies, waits for them, and re-layouts: 3.86 us -> 6.8 us
    dot_general x2 -> x0, matrix products: 2.52 us -> none  [the longest x1 1.47 us: on_device(): jnp.einsum('sr,sw->rw', send_table, column_features, preferred_element_ty...]
  transfers between devices with their start and end apart: 1 -> 0, of which waited for: 1 -> 0; matrix products, arithmetic and copies ran while one was open for 0% -> 0% of each run, Pallas kernels for 0% -> 0%
where the time goes in v3:
time: 120 us
  Pallas kernels  111 us (92%)
  local copies, waits for them, and re-layouts  8.19 us (7%)
    pallas_call x1, Pallas kernels, on_device(): pl.pallas_call(functools.partial(core_kernel, count_x, count_y, capacity,...  111 us
    unnamed x8, local copies, waits for them, and re-layouts  6.8 us

profile of v3, /device:TPU:1, one launch (start us, length us, event | category | flops | bytes accessed | tf_op | source)
XLA Modules:
  0.0 119.8 jit_solution(16656088459904428622)
XLA Ops:
  0.6 1.4 %copy.9.route_col_ref = s32[128,1]{1,0:T(8,128)} copy(s32[128,1]{0,1:T(1,128)} %bitcast.6) | data formatting | bytes 1024 | tf_op jit(solution)/shard_map/broadcast_in_dim | solution.py:622
  2.0 110.9 %shard_map.84 = (bf16[256,1536]{1,0:T(8,128)(2,1)}, bf16[128,1536]{1,0:T(8,128)(2,1)}, f32[27,96,96]{2,1,0:T(8,128)}, f32[27,96,96]{2,1,0:T(8,128)}) custom-call(bf16[128,1536]{1,0:T(8,128)(2,1)} %feat_ref.1, s32[1,128]{1,0:T(1,128)} %bitcast.7, s32[128,1]{1,0:T(8,128)} %copy.9.route_col_ref, bf16[256,1536]{1,0:T(8,128)(2,1)} %bitcast.5, ...), custom_call_target="tpu_custom_call" | custom-call | tf_op jit(solution)/shard_map/pallas_call | solution.py:588
  113.0 0.0 copy-start.1
  113.0 2.2 %copy.14 = bf16[16,16,1536]{2,1,0:T(8,128)(2,1)} copy(bf16[16,16,1536]{2,1,0:T(8,128)(2,1)} %bitcast.4) | data formatting | bytes 1572864
  115.1 1.8 %copy.15 = bf16[128,1536]{1,0:T(8,128)(2,1)} copy(bf16[128,1536]{1,0:T(8,128)(2,1)} %get-tuple-element.17) | data formatting | bytes 786432
  116.9 0.0 copy-done.1
  116.9 0.0 copy-start
  116.9 1.1 copy.16
  118.0 0.7 copy-done
  118.7 1.1 copy.17
Async XLA Ops:
  113.0 3.9 %copy-start.1 = (f32[27,96,96]{2,1,0:T(8,128)S(1)}, f32[27,96,96]{2,1,0:T(8,128)}, u32[]{:S(2)}) copy-start(f32[27,96,96]{2,1,0:T(8,128)} %get-tuple-element.18) | copy-start | bytes 2985988
  116.9 1.8 %copy-start = (f32[27,96,96]{2,1,0:T(8,128)S(1)}, f32[27,96,96]{2,1,0:T(8,128)}, u32[]{:S(2)}) copy-start(f32[27,96,96]{2,1,0:T(8,128)} %get-tuple-element.19) | copy-start | bytes 2985988

commit v4 on v3

--- a/solution.py
+++ b/solution.py
@@ -279,13 +279,13 @@
 
 
 def core_kernel(
-    nx, ny, capacity, factor,
-    feat_ref, route_row_ref, route_col_ref, cot_ref, w1_ref, w2_ref,
-    out_ref, fg_ref, dw1_ref, dw2_ref,
+    nx, ny, capacity,
+    feat_ref, route_row_ref, cot_ref, w1_ref, w2_ref,
+    out_ref, fg_ref, sum_ref,
     x3, g3, a3, h3, tx, tg, ta, th, move, s1, s2, mask_p, turned, grads,
     packed, shares, spread, whole,
     sent, got, back_sent, back_got, routes,
-    halo_send, halo_recv, sum_send, sum_recv, col_send, col_recv,
+    halo_send, halo_recv, sum_send, sum_recv, pair_send, pair_recv, col_send, col_recv,
 ):
     ix, iy = lax.axis_index("rx"), lax.axis_index("ry")
     count = nx * ny
@@ -318,7 +318,8 @@
     ]
     inside = (pl.ds(1, count_x), pl.ds(1, count_y))
 
-    row, col = route_row_ref[...], route_col_ref[...]
+    row = route_row_ref[...]
+    col = jnp.broadcast_to(row.astype(F32), (shard, shard)).T[:, :1].astype(jnp.int32)
     owner_row, owner_col = lax.div(row, slots), lax.div(col, slots)
     same = owner_col == owner_row
     s0, s1_ = iota((shard, shard), 0), iota((shard, shard), 1)
@@ -404,11 +405,20 @@
     halos[1].start()
     shift_inside(g3)
     pair_weights(w1_ref, tx, True)
-    pair_weights(w2_ref, ta, True)
-    pair_weights(w1_ref, th, False)
     halos[1].wait()
     shift_border(g3)
 
+    def conv_to(planes, table, dest):
+        def body(xp, carry):
+            both = pair_conv(planes, table, xp, count_y)
+            for p in range(2):
+                at = pl.ds(pl.multiple_of((2 * xp + p) * rows, rows), rows)
+                dest[at, :] = both[:, p * LANES : (p + 1) * LANES]
+            return carry
+
+        lax.fori_loop(0, count_x // 2, body, 0)
+
+    conv_to(g3, tg, s2)
     wait_all(got, col_recv.at[1])
     arrived = read_messages(got, s1, capacity)
     field_rows = jnp.dot(hot.astype(BF16), arrived, preferred_element_type=F32).astype(BF16)
@@ -416,20 +426,19 @@
     x3[1, inside[0], inside[1]] = s1[...].astype(BF16).reshape(count_x, count_y, depth, LANES)
     halos[0].start()
     shift_inside(x3)
-
-    def conv_to(planes, table, dest):
-        def body(xp, carry):
-            both = pair_conv(planes, table, xp, count_y)
-            for p in range(2):
-                at = pl.ds(pl.multiple_of((2 * xp + p) * rows, rows), rows)
-                dest[at, :] = both[:, p * LANES : (p + 1) * LANES]
-            return carry
-
-        lax.fori_loop(0, count_x // 2, body, 0)
-
-    conv_to(g3, tg, s2)
+    pair_weights(w2_ref, ta, True)
+    pair_weights(w1_ref, th, False)
     halos[0].wait()
     shift_border(x3)
+
+    z_of = iota((rows, LANES), 0) % depth
+
+    def store_shifted(planes, x, v):
+        shape = (count_y, depth, LANES)
+        below = jnp.where(z_of == 0, 0.0, pltpu.roll(v, 1, 0))
+        above = jnp.where(z_of == depth - 1, 0.0, pltpu.roll(v, rows - 1, 0))
+        for c, part in enumerate((below, v, above)):
+            planes[c, x, 1 : count_y + 1] = part.astype(BF16).reshape(shape)
 
     def forward(xp, carry):
         hidden2 = pair_conv(x3, tx, xp, count_y)
@@ -439,11 +448,8 @@
             mask = mask_p[at, :]
             hidden = mask * hidden2[:, p * LANES : (p + 1) * LANES]
             s = 1.0 / (1.0 + jnp.exp(-hidden))
-            a3[1, x + 1, 1 : count_y + 1] = (
-                (hidden * s).astype(BF16).reshape(count_y, depth, LANES)
-            )
-            hg = mask * s2[at, :] * s * (1.0 + hidden * (1.0 - s))
-            h3[1, x + 1, 1 : count_y + 1] = hg.astype(BF16).reshape(count_y, depth, LANES)
+            store_shifted(a3, x + 1, hidden * s)
+            store_shifted(h3, x + 1, mask * s2[at, :] * s * (1.0 + hidden * (1.0 - s)))
         return carry
 
     lax.fori_loop(0, count_x // 2, forward, 0)
@@ -451,16 +457,21 @@
     halos[2].start()
     used = 27 * channels * channels // LANES
     packed[used:, :] = jnp.zeros((packed.shape[0] - used, LANES), F32)
-
-    def sum_out(half, local, planes, flip):
+    core, chip = lax.rem(ix, 2), lax.div(ix, 2) * ny + iy
+    chips = count // 2
+
+    def share_of(other):
+        ox, oy = lax.div(other, ny), lax.rem(other, ny)
+        return lax.rem(ox, 2) * chips + lax.div(ox, 2) * ny + oy
+
+    def send_shares(half, local, planes, flip):
         correlate(local, planes, turned, grads)
         pack_grads(grads, packed, 0, flip, channels)
         shares[half] = packed[...].astype(BF16).reshape(shares.shape[1:])
 
         def send_share(d, carry):
-            other = lax.rem(me + d, count)
             pltpu.make_async_remote_copy(
-                src_ref=shares.at[half, other],
+                src_ref=shares.at[half, share_of(lax.rem(me + d, count))],
                 dst_ref=spread.at[half, d],
                 send_sem=sum_send.at[half],
                 recv_sem=sum_recv.at[half],
@@ -471,10 +482,47 @@
 
         lax.fori_loop(1, count, send_share, 0)
 
-    sum_out(0, h3, x3, False)
-    sum_out(1, a3, g3, True)
-    shift_inside(h3)
-    shift_inside(a3)
+    def send_totals(half):
+        wait_all(spread.at[half], sum_recv.at[half])
+        mine = core * chips + chip
+        total = lax.fori_loop(
+            1,
+            count,
+            lambda d, acc: acc + spread[half, d].astype(F32),
+            shares[half, mine].astype(F32),
+        )
+        whole[half, mine] = total.astype(BF16)
+
+        def send_total(j, carry):
+            other = lax.rem(chip + j, chips)
+            pltpu.make_async_remote_copy(
+                src_ref=whole.at[half, mine],
+                dst_ref=whole.at[half, mine],
+                send_sem=sum_send.at[2 + half],
+                recv_sem=sum_recv.at[2 + half],
+                device_id=(lax.div(other, ny) * 2 + core, lax.rem(other, ny)),
+                device_id_type=mesh_id,
+            ).start()
+            return carry
+
+        lax.fori_loop(1, chips, send_total, 0)
+
+    def across(half):
+        mine = whole.at[half, pl.ds(core * chips, chips)]
+        return pltpu.make_async_remote_copy(
+            src_ref=mine,
+            dst_ref=mine,
+            send_sem=pair_send.at[half],
+            recv_sem=pair_recv.at[half],
+            device_id=(ix + 1 - 2 * core, iy),
+            device_id_type=mesh_id,
+        )
+
+    def wait_same_core(half, sem):
+        part = whole.at[half, pl.ds(0, chips - 1)]
+        pltpu.make_async_copy(part, part, sem).wait()
+
+    send_shares(0, h3, x3, False)
     halos[3].wait()
     shift_border(h3)
 
@@ -513,28 +561,8 @@
         return carry
 
     lax.fori_loop(1, count, send_back, 0)
-
-    for half in range(2):
-        wait_all(spread.at[half], sum_recv.at[half])
-        own_share = shares[half, me].astype(F32)
-        total = lax.fori_loop(
-            1, count, lambda d, acc: acc + spread[half, d].astype(F32), own_share
-        )
-        whole[half, me] = total.astype(BF16)
-
-        def send_total(d, carry):
-            pltpu.make_async_remote_copy(
-                src_ref=whole.at[half, me],
-                dst_ref=whole.at[half, me],
-                send_sem=sum_send.at[2 + half],
-                recv_sem=sum_recv.at[2 + half],
-                device_id=peer(d),
-                device_id_type=mesh_id,
-            ).start()
-            return carry
-
-        lax.fori_loop(1, count, send_total, 0)
-
+    send_shares(1, a3, g3, True)
+    send_totals(0)
     halos[2].wait()
     shift_border(a3)
 
@@ -548,22 +576,36 @@
         return carry
 
     lax.fori_loop(0, count_x // 2, block_body, 0)
+    send_totals(1)
+    wait_same_core(0, sum_recv.at[2])
+    across(0).start()
     out_ref[...] = gather_columns(s1, move, slots, depth)
-
     wait_all(back_got, col_recv.at[2])
     returned = read_messages(back_got, s2, capacity)
     fg_ref[...] = jnp.dot(return_hot, returned, preferred_element_type=F32).astype(BF16)
-
-    for half, dest in enumerate((dw1_ref, dw2_ref)):
-        wait_all(whole.at[half], sum_recv.at[2 + half])
-        packed[...] = whole[half].astype(F32).reshape(packed.shape)
-        unpack_grads(packed, dest, 0, factor, channels)
+    wait_same_core(1, sum_recv.at[3])
+    across(1).start()
     wait_all(routes, col_send.at[0])
     wait_all(got, col_send.at[1])
     wait_all(back_got, col_send.at[2])
+    across(0).wait()
+    sum_ref[0] = whole[0]
+    across(1).wait()
+    sum_ref[1] = whole[1]
     for half in range(2):
         wait_all(spread.at[half], sum_send.at[half])
-        wait_all(whole.at[half], sum_send.at[2 + half])
+        wait_same_core(half, sum_send.at[2 + half])
+
+
+def finish_kernel(
+    factor, out_in, fg_in, sum_ref, out_ref, fg_ref, dw1_ref, dw2_ref, packed
+):
+    out_ref[...] = out_in[...].reshape(out_ref.shape)
+    fg_ref[...] = fg_in[...]
+    channels = dw1_ref.shape[1]
+    for half, dest in enumerate((dw1_ref, dw2_ref)):
+        packed[...] = sum_ref[half].astype(F32).reshape(packed.shape)
+        unpack_grads(packed, dest, 0, factor, channels)
 
 
 def on_device(column_features, column_route, cotangent, first_weight, second_weight):
@@ -585,16 +627,18 @@
     messages = pltpu.VMEM((count_all, capacity * row_width // LANES, LANES), BF16)
     factor = float(1.0 / (count_all * shard_rows * depth) ** 0.5)
     grad_shape = jax.ShapeDtypeStruct((27, channels, channels), F32)
-    out_rows, feature_grads, first_grad, second_grad = pl.pallas_call(
-        functools.partial(core_kernel, count_x, count_y, capacity, factor),
+    vmem = pl.BlockSpec(memory_space=pltpu.VMEM)
+    rows_shape = jax.ShapeDtypeStruct((region_slots, row_width), BF16)
+    back_shape = jax.ShapeDtypeStruct((shard_rows, row_width), BF16)
+    out_rows, back_rows, sums = pl.pallas_call(
+        functools.partial(core_kernel, count_x, count_y, capacity),
         out_shape=(
-            jax.ShapeDtypeStruct((region_slots, row_width), BF16),
-            jax.ShapeDtypeStruct((shard_rows, row_width), BF16),
-            grad_shape,
-            grad_shape,
+            rows_shape,
+            back_shape,
+            jax.ShapeDtypeStruct(share.shape, BF16),
         ),
-        in_specs=[pl.BlockSpec(memory_space=pltpu.VMEM)] * 6,
-        out_specs=[pl.BlockSpec(memory_space=pltpu.VMEM)] * 4,
+        in_specs=[vmem] * 5,
+        out_specs=[vmem] * 3,
         scratch_shapes=[
             planes, planes, planes, planes,
             table, table, table, table,
@@ -610,6 +654,8 @@
             pltpu.SemaphoreType.DMA((4, len(SIDES))),
             pltpu.SemaphoreType.DMA((4,)),
             pltpu.SemaphoreType.DMA((4,)),
+            pltpu.SemaphoreType.DMA((2,)),
+            pltpu.SemaphoreType.DMA((2,)),
             pltpu.SemaphoreType.DMA((3,)),
             pltpu.SemaphoreType.DMA((3,)),
         ],
@@ -619,17 +665,23 @@
     )(
         column_features,
         column_route[None, :],
-        column_route[:, None],
         cotangent.reshape(region_slots, row_width),
         first_weight,
         second_weight,
     )
-    return (
-        out_rows.reshape(region_x, region_y, row_width),
-        feature_grads,
-        first_grad,
-        second_grad,
-    )
+    return pl.pallas_call(
+        functools.partial(finish_kernel, factor),
+        out_shape=(
+            jax.ShapeDtypeStruct(cotangent.shape, BF16),
+            back_shape,
+            grad_shape,
+            grad_shape,
+        ),
+        in_specs=[vmem] * 3,
+        out_specs=[vmem] * 4,
+        scratch_shapes=[pltpu.VMEM((padded, LANES), F32)],
+        compiler_params=params(),
+    )(out_rows, back_rows, sums)
 
 
 def solution(mesh):

time: 120 us -> 116 us (0.967)
  local copies, waits for them, and re-layouts: 8.19 us -> 0 us
  Pallas kernels: 111 us -> 115 us
    unnamed x8 -> x0, local copies, waits for them, and re-layouts: 6.8 us -> none
    pallas_call x1 -> x2, Pallas kernels: 111 us -> 115 us  [the longest x1 107 us: on_device(): pl.pallas_call(functools.partial(core_kernel, count_x, count_y, capacity)...]
    broadcast_in_dim x1 -> x0, local copies, waits for them, and re-layouts: 1.39 us -> none  [on_device(): column_route[:, None]]
where the time goes in v4:
time: 116 us
  Pallas kernels  115 us (99%)
    pallas_call x1, Pallas kernels, on_device(): pl.pallas_call(functools.partial(core_kernel, count_x, count_y, capacity)...  107 us
    pallas_call x1, Pallas kernels, on_device(): pl.pallas_call(functools.partial(finish_kernel, factor), out_shape=(jax.S...  7.92 us

profile of v4, /device:TPU:1, one launch (start us, length us, event | category | flops | bytes accessed | tf_op | source)
XLA Modules:
  0.0 116.0 jit_solution(13820510258376340711)
XLA Ops:
  0.6 107.5 %shard_map.84 = (bf16[256,1536]{1,0:T(8,128)(2,1)}, bf16[128,1536]{1,0:T(8,128)(2,1)}, bf16[2,128,16,128]{3,2,1,0:T(8,128)(2,1)}) custom-call(bf16[128,1536]{1,0:T(8,128)(2,1)} %feat_ref.1, s32[1,128]{1,0:T(1,128)} %bitcast.3, bf16[256,1536]{1,0:T(8,128)(2,1)} %bitcast.2, bf16[27,96,96]{2,1,0:T(8,128)(2,1)} %w1_ref.1, bf16[27,96,96]{2,1,0:T(8,128)(2,1)} %w2_ref.1), custom_call_target="tpu_custom_call" | custom-call | tf_op jit(solution)/shard_map/pallas_call | solution.py:633
  108.1 7.9 %shard_map.85 = (bf16[16,16,1536]{2,1,0:T(8,128)(2,1)}, bf16[128,1536]{1,0:T(8,128)(2,1)}, f32[27,96,96]{2,1,0:T(8,128)}, f32[27,96,96]{2,1,0:T(8,128)}) custom-call(bf16[256,1536]{1,0:T(8,128)(2,1)} %get-tuple-element.7.out_in, bf16[128,1536]{1,0:T(8,128)(2,1)} %get-tuple-element.8.fg_in, bf16[2,128,16,128]{3,2,1,0:T(8,128)(2,1)} %get-tuple-element.9.sum_ref), custom_call_target="tpu_custom_call" | custom-call | tf_op jit(solution)/shard_map/pallas_call | solution.py:672

commit v5 on v4

--- a/solution.py
+++ b/solution.py
@@ -168,7 +168,7 @@
     rest = channels - tall
     lane = iota((tall, LANES), 1)
 
-    def body(k, carry):
+    def body(k):
         block = out[9 + 26 - k].T if flip else out[9 + k]
         low = block[tall:channels]
         part = LANES - channels
@@ -177,9 +177,13 @@
         )
         at = pl.ds(pl.multiple_of((base + k) * tall, 8), tall)
         packed[at, :] = jnp.where(lane < channels, block[:tall], moved)
+
+    def three(step, carry):
+        for t in range(3):
+            body(3 * step + t)
         return carry
 
-    lax.fori_loop(0, 27, body, 0)
+    lax.fori_loop(0, 9, three, 0)
 
 
 def unpack_grads(packed, dest, base, factor, channels):
@@ -188,7 +192,7 @@
     part = LANES - channels
     lane = iota((rest, LANES), 1)
 
-    def body(k, carry):
+    def body(k):
         v = packed[pl.ds(pl.multiple_of((base + k) * tall, 8), tall), :] * factor
         low = jnp.zeros((rest, LANES), F32)
         for m in range(tall // rest):
@@ -196,9 +200,13 @@
             low = jnp.where(lane // part == m, turned, low)
         dest[k, :tall, :] = v[:, :channels]
         dest[k, tall:, :] = low[:, :channels]
+
+    def three(step, carry):
+        for t in range(3):
+            body(3 * step + t)
         return carry
 
-    lax.fori_loop(0, 27, body, 0)
+    lax.fori_loop(0, 9, three, 0)
 
 
 class Halo:
@@ -293,18 +301,34 @@
     barrier = pltpu.get_barrier_semaphore()
     mesh_id = pl.DeviceIdType.MESH
 
-    def peer(d):
-        other = lax.rem(me + d, count)
-        return (lax.div(other, ny), lax.rem(other, ny))
+    def wrap(value, extent):
+        value = jnp.where(value >= extent, value - extent, value)
+        return jnp.where(value < 0, value + extent, value)
+
+    def each_peer(visit, stride=1, way=1):
+        for dx in range(0, nx, stride):
+            px = wrap(ix + way * dx, nx)
+
+            def single(dy):
+                visit(dx * ny + dy, px, wrap(iy + way * dy, ny))
+
+            def four(step, carry):
+                for k in range(4):
+                    single(4 * step + k)
+                return carry
+
+            if dx == 0:
+                for dy in range(1, 4):
+                    single(dy)
+            lax.fori_loop(1 if dx == 0 else 0, ny // 4, four, 0)
 
     for planes in (x3, g3, a3, h3):
         clear_border(planes)
 
-    def greet(d, carry):
-        pl.semaphore_signal(barrier, inc=1, device_id=peer(d), device_id_type=mesh_id)
-        return carry
-
-    lax.fori_loop(1, count, greet, 0)
+    def greet(d, px, py):
+        pl.semaphore_signal(barrier, inc=1, device_id=(px, py), device_id_type=mesh_id)
+
+    each_peer(greet)
     _, count_x, count_y, depth, _ = x3.shape
     count_x, count_y = count_x - 2, count_y - 2
     rows = count_y * depth
@@ -325,8 +349,12 @@
     s0, s1_ = iota((shard, shard), 0), iota((shard, shard), 1)
     rank_row = jnp.sum(jnp.where(same & (s0 < s1_), 1.0, 0.0), axis=0, keepdims=True)
     rank_col = jnp.sum(jnp.where(same & (s1_ < s0), 1.0, 0.0), axis=1, keepdims=True)
-    ahead_row = lax.rem(owner_row - me + count, count)
-    ahead_col = lax.rem(owner_col - me + count, count)
+
+    def ahead(owner):
+        far = lax.rem(lax.div(owner, ny) - ix + nx, nx)
+        return far * ny + lax.rem(lax.rem(owner, ny) - iy + ny, ny)
+
+    ahead_row, ahead_col = ahead(owner_row), ahead(owner_col)
     place_row = rank_row.astype(jnp.int32) * count + ahead_row
     place_col = rank_col.astype(jnp.int32) * count + ahead_col
     buffer = capacity * count
@@ -346,33 +374,31 @@
     got[0] = sent[0]
     pl.semaphore_wait(barrier, count - 1)
 
-    def send_route(d, carry):
+    def send_route(d, px, py):
         pltpu.make_async_remote_copy(
             src_ref=route_row_ref,
             dst_ref=routes.at[d],
             send_sem=col_send.at[0],
             recv_sem=col_recv.at[0],
-            device_id=peer(d),
+            device_id=(px, py),
             device_id_type=mesh_id,
         ).start()
-        return carry
-
-    def send_column(d, carry):
+
+    def send_column(d, px, py):
         pltpu.make_async_remote_copy(
             src_ref=sent.at[d],
             dst_ref=got.at[d],
             send_sem=col_send.at[1],
             recv_sem=col_recv.at[1],
-            device_id=peer(d),
+            device_id=(px, py),
             device_id_type=mesh_id,
         ).start()
-        return carry
 
     def wait_all(ref, sem):
         pltpu.make_async_copy(ref.at[pl.ds(1, count - 1)], ref.at[pl.ds(1, count - 1)], sem).wait()
 
-    lax.fori_loop(1, count, send_route, 0)
-    lax.fori_loop(1, count, send_column, 0)
+    each_peer(send_route)
+    each_peer(send_column)
 
     build_move(move, depth)
     spread_columns(cot_ref[...], None, move, s2, depth)
@@ -460,52 +486,44 @@
     core, chip = lax.rem(ix, 2), lax.div(ix, 2) * ny + iy
     chips = count // 2
 
-    def share_of(other):
-        ox, oy = lax.div(other, ny), lax.rem(other, ny)
-        return lax.rem(ox, 2) * chips + lax.div(ox, 2) * ny + oy
+    def share_of(px, py):
+        return lax.rem(px, 2) * chips + lax.div(px, 2) * ny + py
 
     def send_shares(half, local, planes, flip):
         correlate(local, planes, turned, grads)
         pack_grads(grads, packed, 0, flip, channels)
         shares[half] = packed[...].astype(BF16).reshape(shares.shape[1:])
 
-        def send_share(d, carry):
+        def send_share(d, px, py):
             pltpu.make_async_remote_copy(
-                src_ref=shares.at[half, share_of(lax.rem(me + d, count))],
+                src_ref=shares.at[half, share_of(px, py)],
                 dst_ref=spread.at[half, d],
                 send_sem=sum_send.at[half],
                 recv_sem=sum_recv.at[half],
-                device_id=peer(d),
+                device_id=(px, py),
                 device_id_type=mesh_id,
             ).start()
-            return carry
-
-        lax.fori_loop(1, count, send_share, 0)
+
+        each_peer(send_share)
 
     def send_totals(half):
         wait_all(spread.at[half], sum_recv.at[half])
         mine = core * chips + chip
-        total = lax.fori_loop(
-            1,
-            count,
-            lambda d, acc: acc + spread[half, d].astype(F32),
-            shares[half, mine].astype(F32),
-        )
+        total = shares[half, mine].astype(F32)
+        total = total + jnp.sum(spread[half, 1:].astype(F32), axis=0)
         whole[half, mine] = total.astype(BF16)
 
-        def send_total(j, carry):
-            other = lax.rem(chip + j, chips)
+        def send_total(d, px, py):
             pltpu.make_async_remote_copy(
                 src_ref=whole.at[half, mine],
                 dst_ref=whole.at[half, mine],
                 send_sem=sum_send.at[2 + half],
                 recv_sem=sum_recv.at[2 + half],
-                device_id=(lax.div(other, ny) * 2 + core, lax.rem(other, ny)),
+                device_id=(px, py),
                 device_id_type=mesh_id,
             ).start()
-            return carry
-
-        lax.fori_loop(1, chips, send_total, 0)
+
+        each_peer(send_total, stride=2)
 
     def across(half):
         mine = whole.at[half, pl.ds(core * chips, chips)]
@@ -549,18 +567,17 @@
     )
     back_got[0] = back_sent[0]
 
-    def send_back(d, carry):
+    def send_back(d, px, py):
         pltpu.make_async_remote_copy(
             src_ref=back_sent.at[d],
             dst_ref=back_got.at[d],
             send_sem=col_send.at[2],
             recv_sem=col_recv.at[2],
-            device_id=peer(count - d),
+            device_id=(px, py),
             device_id_type=mesh_id,
         ).start()
-        return carry
-
-    lax.fori_loop(1, count, send_back, 0)
+
+    each_peer(send_back, way=-1)
     send_shares(1, a3, g3, True)
     send_totals(0)
     halos[2].wait()
@@ -598,14 +615,38 @@
 
 
 def finish_kernel(
-    factor, out_in, fg_in, sum_ref, out_ref, fg_ref, dw1_ref, dw2_ref, packed
+    factor,
+    out_in, fg_in, sum_in,
+    out_ref, fg_ref, dw1_ref, dw2_ref,
+    v_out, v_fg, v_sum, grads1, grads2, packed, sems,
 ):
-    out_ref[...] = out_in[...].reshape(out_ref.shape)
-    fg_ref[...] = fg_in[...]
-    channels = dw1_ref.shape[1]
-    for half, dest in enumerate((dw1_ref, dw2_ref)):
-        packed[...] = sum_ref[half].astype(F32).reshape(packed.shape)
+    copies = [
+        pltpu.make_async_copy(source, dest, sems.at[k])
+        for k, (source, dest) in enumerate(
+            (
+                (sum_in.at[0], v_sum.at[0]),
+                (sum_in.at[1], v_sum.at[1]),
+                (out_in, v_out),
+                (fg_in, v_fg),
+                (v_out, out_ref),
+                (v_fg, fg_ref),
+                (grads1, dw1_ref),
+                (grads2, dw2_ref),
+            )
+        )
+    ]
+    for copy in copies[:4]:
+        copy.start()
+    channels = grads1.shape[1]
+    for half, dest in enumerate((grads1, grads2)):
+        copies[half].wait()
+        packed[...] = v_sum[half].astype(F32).reshape(packed.shape)
         unpack_grads(packed, dest, 0, factor, channels)
+        copies[6 + half].start()
+        copies[2 + half].wait()
+        copies[4 + half].start()
+    for copy in copies[4:]:
+        copy.wait()
 
 
 def on_device(column_features, column_route, cotangent, first_weight, second_weight):
@@ -669,19 +710,24 @@
         first_weight,
         second_weight,
     )
-    return pl.pallas_call(
+    anywhere = pl.BlockSpec(memory_space=pl.ANY)
+    out_rows, feature_grads, first_grad, second_grad = pl.pallas_call(
         functools.partial(finish_kernel, factor),
-        out_shape=(
-            jax.ShapeDtypeStruct(cotangent.shape, BF16),
-            back_shape,
-            grad_shape,
-            grad_shape,
-        ),
-        in_specs=[vmem] * 3,
-        out_specs=[vmem] * 4,
-        scratch_shapes=[pltpu.VMEM((padded, LANES), F32)],
+        out_shape=(rows_shape, back_shape, grad_shape, grad_shape),
+        in_specs=[anywhere] * 3,
+        out_specs=[anywhere] * 4,
+        scratch_shapes=[
+            pltpu.VMEM(rows_shape.shape, BF16),
+            pltpu.VMEM(back_shape.shape, BF16),
+            pltpu.VMEM(share.shape, BF16),
+            pltpu.VMEM(grad_shape.shape, F32),
+            pltpu.VMEM(grad_shape.shape, F32),
+            pltpu.VMEM((padded, LANES), F32),
+            pltpu.SemaphoreType.DMA((8,)),
+        ],
         compiler_params=params(),
     )(out_rows, back_rows, sums)
+    return out_rows.reshape(cotangent.shape), feature_grads, first_grad, second_grad
 
 
 def solution(mesh):

time: 116 us -> 105 us (0.905)
  Pallas kernels: 115 us -> 104 us
    pallas_call x1, Pallas kernels: 107 us -> 99.8 us  [on_device(): pl.pallas_call(functools.partial(core_kernel, count_x, count_y, capacity)...]
    pallas_call x1, Pallas kernels: 7.92 us -> 4.23 us  [on_device(): pl.pallas_call(functools.partial(finish_kernel, factor), out_shape=(rows_...]
where the time goes in v5:
time: 105 us
  Pallas kernels  104 us (99%)
    pallas_call x1, Pallas kernels, on_device(): pl.pallas_call(functools.partial(core_kernel, count_x, count_y, capacity)...  99.8 us
    pallas_call x1, Pallas kernels, on_device(): pl.pallas_call(functools.partial(finish_kernel, factor), out_shape=(rows_...  4.23 us

profile of v5, /device:TPU:1, one launch (start us, length us, event | category | flops | bytes accessed | tf_op | source)
XLA Modules:
  0.0 104.9 jit_solution(15287822877377926215)
XLA Ops:
  0.6 99.8 %shard_map.84 = (bf16[256,1536]{1,0:T(8,128)(2,1)}, bf16[128,1536]{1,0:T(8,128)(2,1)}, bf16[2,128,16,128]{3,2,1,0:T(8,128)(2,1)}) custom-call(bf16[128,1536]{1,0:T(8,128)(2,1)} %feat_ref.1, s32[1,128]{1,0:T(1,128)} %bitcast.4, bf16[256,1536]{1,0:T(8,128)(2,1)} %bitcast.3, bf16[27,96,96]{2,1,0:T(8,128)(2,1)} %w1_ref.1, bf16[27,96,96]{2,1,0:T(8,128)(2,1)} %w2_ref.1), custom_call_target="tpu_custom_call" | custom-call | tf_op jit(solution)/shard_map/pallas_call | solution.py:674
  100.4 4.2 %shard_map.85 = (bf16[256,1536]{1,0:T(8,128)(2,1)}, bf16[128,1536]{1,0:T(8,128)(2,1)}, f32[27,96,96]{2,1,0:T(8,128)}, f32[27,96,96]{2,1,0:T(8,128)}) custom-call(bf16[256,1536]{1,0:T(8,128)(2,1)} %get-tuple-element.11.out_in, bf16[128,1536]{1,0:T(8,128)(2,1)} %get-tuple-element.12.fg_in, bf16[2,128,16,128]{3,2,1,0:T(8,128)(2,1)} %get-tuple-element.13.sum_in), custom_call_target="tpu_custom_call" | custom-call | tf_op jit(solution)/shard_map/pallas_call | solution.py:714

commit v6 on v5

--- a/solution.py
+++ b/solution.py
@@ -108,16 +108,27 @@
                     table[row : row + channels, p * LANES : p * LANES + channels] = block
 
 
-def pair_conv(planes, table, xp, count_y):
+def pair_conv(planes, table, step, count_y):
     depth = planes.shape[3]
-    pieces = []
-    for j in range(4):
-        for b in range(3):
-            for c in range(3):
-                pieces.append(
-                    planes[c, 2 * xp + j, b : b + count_y].reshape(count_y * depth, LANES)
-                )
-    return jnp.dot(jnp.concatenate(pieces, axis=1), table[...], preferred_element_type=F32)
+    halves = []
+    for h in range(2):
+        pieces = []
+        for j in range(4):
+            for b in range(3):
+                for c in range(3):
+                    pieces.append(
+                        planes[c, 4 * step + 2 * h + j, b : b + count_y].reshape(
+                            count_y * depth, LANES
+                        )
+                    )
+        halves.append(jnp.concatenate(pieces, axis=1))
+    return jnp.dot(jnp.concatenate(halves, axis=0), table[...], preferred_element_type=F32)
+
+
+def quarter(both, k):
+    rows = both.shape[0] // 2
+    h, p = divmod(k, 2)
+    return both[h * rows : (h + 1) * rows, p * LANES : (p + 1) * LANES]
 
 
 def correlate(local, planes, turned, out):
@@ -437,12 +448,12 @@
     def conv_to(planes, table, dest):
         def body(xp, carry):
             both = pair_conv(planes, table, xp, count_y)
-            for p in range(2):
-                at = pl.ds(pl.multiple_of((2 * xp + p) * rows, rows), rows)
-                dest[at, :] = both[:, p * LANES : (p + 1) * LANES]
+            for p in range(4):
+                at = pl.ds(pl.multiple_of((4 * xp + p) * rows, rows), rows)
+                dest[at, :] = quarter(both, p)
             return carry
 
-        lax.fori_loop(0, count_x // 2, body, 0)
+        lax.fori_loop(0, count_x // 4, body, 0)
 
     conv_to(g3, tg, s2)
     wait_all(got, col_recv.at[1])
@@ -468,17 +479,17 @@
 
     def forward(xp, carry):
         hidden2 = pair_conv(x3, tx, xp, count_y)
-        for p in range(2):
-            x = 2 * xp + p
+        for p in range(4):
+            x = 4 * xp + p
             at = pl.ds(pl.multiple_of(x * rows, rows), rows)
             mask = mask_p[at, :]
-            hidden = mask * hidden2[:, p * LANES : (p + 1) * LANES]
+            hidden = mask * quarter(hidden2, p)
             s = 1.0 / (1.0 + jnp.exp(-hidden))
             store_shifted(a3, x + 1, hidden * s)
             store_shifted(h3, x + 1, mask * s2[at, :] * s * (1.0 + hidden * (1.0 - s)))
         return carry
 
-    lax.fori_loop(0, count_x // 2, forward, 0)
+    lax.fori_loop(0, count_x // 4, forward, 0)
     halos[3].start()
     halos[2].start()
     used = 27 * channels * channels // LANES
@@ -546,14 +557,14 @@
 
     def grad_body(xp, carry):
         both = pair_conv(h3, th, xp, count_y)
-        for p in range(2):
-            x = 2 * xp + p
+        for p in range(4):
+            x = 4 * xp + p
             at = pl.ds(pl.multiple_of(x * rows, rows), rows)
             cot = g3[1, x + 1, 1 : count_y + 1].reshape(rows, LANES).astype(F32)
-            s2[at, :] = cot + both[:, p * LANES : (p + 1) * LANES]
+            s2[at, :] = cot + quarter(both, p)
         return carry
 
-    lax.fori_loop(0, count_x // 2, grad_body, 0)
+    lax.fori_loop(0, count_x // 4, grad_body, 0)
     grad_rows = gather_columns(s2, move, slots, depth)
     back_rows = jnp.dot(back_hot, grad_rows, preferred_element_type=F32)
     lay_messages(
@@ -585,14 +596,14 @@
 
     def block_body(xp, carry):
         both = pair_conv(a3, ta, xp, count_y)
-        for p in range(2):
-            x = 2 * xp + p
+        for p in range(4):
+            x = 4 * xp + p
             at = pl.ds(pl.multiple_of(x * rows, rows), rows)
             own = x3[1, x + 1, 1 : count_y + 1].reshape(rows, LANES).astype(F32)
-            s1[at, :] = own + mask_p[at, :] * both[:, p * LANES : (p + 1) * LANES]
+            s1[at, :] = own + mask_p[at, :] * quarter(both, p)
         return carry
 
-    lax.fori_loop(0, count_x // 2, block_body, 0)
+    lax.fori_loop(0, count_x // 4, block_body, 0)
     send_totals(1)
     wait_same_core(0, sum_recv.at[2])
     across(0).start()

time: 105 us -> 103 us (0.981)
  Pallas kernels: 104 us -> 102 us
    pallas_call x1, Pallas kernels: 99.8 us -> 97.8 us  [on_device(): pl.pallas_call(functools.partial(core_kernel, count_x, count_y, capacity)...]
where the time goes in v6:
time: 103 us
  Pallas kernels  102 us (99%)
    pallas_call x1, Pallas kernels, on_device(): pl.pallas_call(functools.partial(core_kernel, count_x, count_y, capacity)...  97.8 us
    pallas_call x1, Pallas kernels, on_device(): pl.pallas_call(functools.partial(finish_kernel, factor), out_shape=(rows_...  4.23 us

profile of v6, /device:TPU:1, one launch (start us, length us, event | category | flops | bytes accessed | tf_op | source)
XLA Modules:
  0.0 102.8 jit_solution(15865490626705217867)
XLA Ops:
  0.6 97.8 %shard_map.84 = (bf16[256,1536]{1,0:T(8,128)(2,1)}, bf16[128,1536]{1,0:T(8,128)(2,1)}, bf16[2,128,16,128]{3,2,1,0:T(8,128)(2,1)}) custom-call(bf16[128,1536]{1,0:T(8,128)(2,1)} %feat_ref.1, s32[1,128]{1,0:T(1,128)} %bitcast.4, bf16[256,1536]{1,0:T(8,128)(2,1)} %bitcast.3, bf16[27,96,96]{2,1,0:T(8,128)(2,1)} %w1_ref.1, bf16[27,96,96]{2,1,0:T(8,128)(2,1)} %w2_ref.1), custom_call_target="tpu_custom_call" | custom-call | tf_op jit(solution)/shard_map/pallas_call | solution.py:685
  98.4 4.2 %shard_map.85 = (bf16[256,1536]{1,0:T(8,128)(2,1)}, bf16[128,1536]{1,0:T(8,128)(2,1)}, f32[27,96,96]{2,1,0:T(8,128)}, f32[27,96,96]{2,1,0:T(8,128)}) custom-call(bf16[256,1536]{1,0:T(8,128)(2,1)} %get-tuple-element.11.out_in, bf16[128,1536]{1,0:T(8,128)(2,1)} %get-tuple-element.12.fg_in, bf16[2,128,16,128]{3,2,1,0:T(8,128)(2,1)} %get-tuple-element.13.sum_in), custom_call_target="tpu_custom_call" | custom-call | tf_op jit(solution)/shard_map/pallas_call | solution.py:725
